TPU v7x, 256 devices: a whole 4x4x8 slice. The times are simulated.
256 devices in a mesh: pitch: 16 (over x_lo, z), radial: 8 (over y, core), axial: 2 (over x_hi).
Axes of the slice: x: 4 (x_hi: 2, x_lo: 2; x = x_hi * 2 + x_lo), y: 4, z: 8, core: 2. Of those that a mesh axis runs over, the one named last changes fastest.
Arguments:
- density: float32 [9, 4, 64, 2048], P(None, 'axial', 'radial', 'pitch'), may hold values from 0.5 to 2
- moments: float32 [9, 4, 4, 64, 2048], P(None, None, 'axial', 'radial', 'pitch'), may hold values from -6 to 6
- shifts: int32 [9], replicated, may hold values from 0 to 2047, as said below
Outputs:
- residual: float32 [9, 5, 4, 64, 2048], P(None, None, 'axial', 'radial', 'pitch')
- update: float32 [9, 5, 4, 64, 2048], P(None, None, 'axial', 'radial', 'pitch')
Inputs may be any that keep to these rules, and one draw needn't show every extreme that they name: `shifts`: every instance's offset lies in 0 to 2047 and some instance has offset 2048 - 1.
All inputs are finite; a program needn't handle non-finite values.
Results may differ from a plain program's by a relative error of at most 0.0005.
Values sent between devices are 32-bit elements; how exact they have to be, the bound alone decides.
No kernel may reach another device: no remote copies, remote signals or barrier semaphores. Data moves between devices by JAX's collectives and lax.ppermute only.
A program may use at most 192 MiB of HBM per device.

v0:
```python
import math

import jax
import jax.numpy as jnp
import numpy as np
from jax import lax
from jax.sharding import PartitionSpec as P

COEFFS = (0.75, -0.15, 1.0 / 60.0)
GAMMA_LESS = 0.4
HIGHEST = lax.Precision.HIGHEST


def padded_2(x, sides, width, wrap):
    for axis, dim in sides:
        devices, length = (lax.axis_size(axis), x.shape[dim])
        up = [(i, (i + 1) % devices) for i in range(devices if wrap else devices - 1)]
        down = [(j, i) for i, j in up]
        last = lax.slice_in_dim(x, length - width, length, axis=dim)
        leading = lax.slice_in_dim(x, 0, width, axis=dim)
        before = lax.ppermute(last, axis, up)
        after = lax.ppermute(leading, axis, down)
        x = jnp.concatenate([before, x, after], axis=dim)
    return x


def carried_in(x, axis, combine, identity, reverse):
    devices, position = (lax.axis_size(axis), lax.axis_index(axis))
    everything = jax.tree.map(lambda part: lax.all_gather(part, axis), x)
    start = jax.tree.map(
        lambda part, zero: jnp.broadcast_to(jnp.asarray(zero, part.dtype), part.shape), x, identity
    )

    def hop(k, before):
        at = devices - 1 - k if reverse else k
        reached = at > position if reverse else at < position
        new = combine(before, jax.tree.map(lambda part: part[at], everything))
        return jax.tree.map(lambda a, b: jnp.where(reached, a, b), new, before)

    return lax.fori_loop(0, devices, hop, start)


def from_partner(x, axis, apart):
    return lax.ppermute(x, axis, [(i, i ^ 1 << apart) for i in range(lax.axis_size(axis))])


def spectral_table(count):
    points = np.arange(count)
    spread = points[:, None] - points[None, :]
    nonzero = np.where(spread == 0, 1, spread)
    entries = 0.5 * np.where(spread % 2 == 0, 1.0, -1.0) / np.sin(np.pi * nonzero / count)
    return jnp.asarray(np.where(spread == 0, 0.0, entries), jnp.float32)


def fluxes(density, moments):
    axial_m = moments[:, 0]
    radial_m = moments[:, 1]
    pitch_m = moments[:, 2]
    energy = moments[:, 3]
    pressure = GAMMA_LESS * (
        energy - 0.5 * (axial_m * axial_m + radial_m * radial_m + pitch_m * pitch_m) / density
    )
    pitch_v = pitch_m / density
    radial_v = radial_m / density
    along_pitch = jnp.stack(
        [
            pitch_m,
            axial_m * pitch_v,
            radial_m * pitch_v,
            pitch_m * pitch_v + pressure,
            (energy + pressure) * pitch_v,
        ],
        axis=1,
    )
    along_radial = jnp.stack(
        [
            radial_m,
            axial_m * radial_v,
            radial_m * radial_v + pressure,
            pitch_m * radial_v,
            (energy + pressure) * radial_v,
        ],
        axis=1,
    )
    return (along_pitch, along_radial)


def stencil(padded, axis, length):
    summed = None
    for offset, weight in enumerate(COEFFS):
        reach = offset + 1
        ahead = lax.slice_in_dim(padded, 3 + reach, 3 + reach + length, axis=axis)
        behind = lax.slice_in_dim(padded, 3 - reach, 3 - reach + length, axis=axis)
        term = weight * (ahead - behind)
        summed = term if summed is None else summed + term
    return summed


def pitch_derivative(along_pitch):
    width = along_pitch.shape[-1]
    edges = jnp.concatenate([along_pitch[..., :3], along_pitch[..., width - 3 :]], axis=4)
    rims = padded_2(edges, (("pitch", 4),), 3, True)
    inner = None
    for offset, weight in enumerate(COEFFS):
        reach = offset + 1
        term = weight * (
            jnp.roll(along_pitch, -reach, axis=4) - jnp.roll(along_pitch, reach, axis=4)
        )
        inner = term if inner is None else inner + term
    left_strip = jnp.concatenate([rims[..., 0:3], along_pitch[..., :6]], axis=4)
    right_strip = jnp.concatenate([along_pitch[..., width - 6 :], rims[..., 9:12]], axis=4)
    left_cols = stencil(left_strip, 4, 3)
    right_cols = stencil(right_strip, 4, 3)
    pad_none = ((0, 0),) * 4
    left_full = jnp.pad(left_cols, pad_none + ((0, width - 3),))
    right_full = jnp.pad(right_cols, pad_none + ((width - 3, 0),))
    column = jnp.arange(width)
    return jnp.where(column < 3, left_full, jnp.where(column >= width - 3, right_full, inner))


def cut_rows(joined, starts, width):
    pieces = []
    for member in range(joined.shape[0]):
        opening = starts[member]
        pieces.append(lax.dynamic_slice_in_dim(joined[member], opening, width, axis=2))
    return jnp.stack(pieces, axis=0)


def carry_in(sums, backward, width, decay):
    count_p = lax.axis_size("pitch")
    place = lax.axis_index("pitch")
    step_log = width * math.log(decay)
    wrap_gain = 1.0 / (1.0 - decay ** (width * count_p))
    position = count_p - 1 - place if backward else place
    factor = jnp.full((1,), decay**width, jnp.float32)

    def combine(earlier, later):
        return (earlier[0] * later[0], later[1] + later[0] * earlier[1])

    scanned = carried_in(
        (factor, sums),
        "pitch",
        combine,
        (jnp.ones((1,), jnp.float32), jnp.zeros_like(sums)),
        backward,
    )
    weighted = sums * jnp.exp((count_p - 1 - position).astype(jnp.float32) * step_log)
    circuit = lax.psum(weighted, "pitch")
    return scanned[1] + jnp.exp(position.astype(jnp.float32) * step_log) * wrap_gain * circuit


def smooth(residual):
    width = residual.shape[-1]
    extent = width * lax.axis_size("pitch")
    smooth_eps = float(extent * extent // 16)
    decay = 2.0 * smooth_eps / (1.0 + 2.0 * smooth_eps + math.sqrt(1.0 + 4.0 * smooth_eps))
    points = np.arange(width)
    spacing = points[None, :] - points[:, None]
    lower = np.where(spacing >= 0, decay ** np.maximum(spacing, 0), 0.0)
    forward_table = jnp.asarray(lower, jnp.float32)
    backward_table = jnp.asarray(lower.T, jnp.float32)
    rising = jnp.asarray(decay ** (points + 1.0), jnp.float32)
    falling = jnp.asarray(decay ** (width - points + 0.0), jnp.float32)
    flat = residual.reshape(-1, width)
    first_pass = jnp.dot(flat, forward_table, precision=HIGHEST, preferred_element_type=jnp.float32)
    carried = carry_in(first_pass[:, -1], False, width, decay)
    swept = first_pass + carried[:, None] * rising[None, :]
    second_pass = jnp.dot(
        swept, backward_table, precision=HIGHEST, preferred_element_type=jnp.float32
    )
    carried_back = carry_in(second_pass[:, 0], True, width, decay)
    result = (second_pass + carried_back[:, None] * falling[None, :]) * (decay / smooth_eps)
    return result.reshape(residual.shape)


def local(density, moments, shifts):
    fields = jnp.concatenate([density[:, None], moments], axis=1)
    along_pitch, along_radial = fluxes(density, moments)
    count_p = lax.axis_size("pitch")
    place = lax.axis_index("pitch")
    width = density.shape[-1]
    planes = density.shape[1]
    padded_r = padded_2(along_radial, (("radial", 3),), 3, False)
    residual = pitch_derivative(along_pitch) + stencil(padded_r, 3, density.shape[2])
    residual = residual + jnp.einsum(
        "nm,mvarp->nvarp", spectral_table(fields.shape[0]), fields, precision=HIGHEST
    )
    stator = lax.axis_index("axial") == 1
    edge = jnp.where(stator, fields[:, :, 0], fields[:, :, planes - 1])
    facing = from_partner(edge, "axial", 0)
    extent = width * count_p
    offsets = jnp.where(stator, shifts, (extent - shifts) % extent)
    whole = lax.all_gather(facing, "pitch", axis=3, tiled=True)
    joined = jnp.concatenate([whole, whole], axis=3)
    aligned = cut_rows(joined, (place * width - offsets) % extent, width)
    penalty = aligned - edge
    target = jnp.where(stator, 0, planes - 1)
    chosen = (jnp.arange(planes) == target).astype(jnp.float32)
    residual = residual + penalty[:, :, None] * chosen[None, None, :, None, None]
    update = smooth(residual)
    return (residual, update)


def solution(mesh):
    in_specs = (P(None, "axial", "radial", "pitch"), P(None, None, "axial", "radial", "pitch"), P())
    out_specs = (
        P(None, None, "axial", "radial", "pitch"),
        P(None, None, "axial", "radial", "pitch"),
    )
    return jax.shard_map(local, mesh=mesh, in_specs=in_specs, out_specs=out_specs, check_vma=False)
```

profile of v0, /device:TPU:8, one launch (start us, length us, event | category | flops | bytes accessed | tf_op | source)
XLA Modules:
  0.0 391.4 jit_solution(6950493124615744178)
XLA Ops:
  7.2 1.1 copy.155
  8.4 1.0 copy.166
  9.4 3.1 collective-permute-start.4
  12.5 1.7 fusion.59
  14.2 1.3 copy.143
  15.9 1.1 constant_dynamic-update-slice_fusion
  17.0 1.3 copy.162
  18.3 1.3 copy.163
  19.6 1.1 constant_dynamic-update-slice_fusion.1
  20.6 2.4 fusion.24
  23.0 2.2 copy.146
  25.2 2.4 bitcast_dynamic-update-slice_fusion.7
  27.6 2.8 bitcast_dynamic-update-slice_fusion.6
  30.4 0.7 multiply_divide_fusion
  31.1 2.2 copy.148
  33.3 1.4 copy.164
  34.7 2.9 bitcast_dynamic-update-slice_fusion.5
  38.2 3.0 bitcast_dynamic-update-slice_fusion.4
  41.2 1.7 fusion.52
  42.9 1.9 collective-permute-start
  44.8 4.0 %collective-permute-start.1 = (f32[9,5,2,8,3]{0,3,4,2,1:T(8,128)}, f32[9,5,2,8,3]{0,3,4,2,1:T(8,128)}, u32[]{:S(2)}, u32[]{:S(2)}) collective-permute-start(f32[9,5,2,8,3]{0,3,4,2,1:T(8,128)} %get-tuple-element.323), channel_id=1, source_target_pairs={{16,0},{32,16},{48,32},{64,48},{80,64},{96,80},{112,96},{128,112},... | collective-permute-start | bytes 25928 | tf_op jit(solution)/shard_map/ppermute | solution.py:22
  49.3 2.3 copy-done.1
  51.6 2.6 fusion.58
  54.1 3.5 copy.150
  57.6 1.9 collective-permute-start.2
  59.6 2.2 copy.152
  61.8 2.4 collective-permute-start.3
  64.8 0.7 fusion.60
  65.5 1.4 fusion.56
  66.9 1.6 fusion.54
  68.5 1.6 fusion.27
  70.1 1.3 fusion.51
  71.4 8.8 %fusion.53 = (f32[9,5,2,8,125]{0,3,4,2,1:T(8,128)}, f32[9,5,2,8,125]{0,3,4,2,1:T(8,128)}) fusion(f32[9,5,2,8,128]{0,3,4,2,1:T(8,128)} %get-tuple-element.336), kind=kLoop, calls=%fused_computation.138 | loop fusion | bytes 1440000 | tf_op jit(solution)/shard_map/jit(_roll_static)/slice | solution.py:107
  80.2 4.7 %fusion.55 = (f32[9,5,2,8,126]{0,3,4,2,1:T(8,128)}, f32[9,5,2,8,126]{0,3,4,2,1:T(8,128)}) fusion(f32[9,5,2,8,128]{0,3,4,2,1:T(8,128)S(1)} %bitcast.139), kind=kLoop, calls=%fused_computation.140 | loop fusion | bytes 1451520 | tf_op jit(solution)/shard_map/jit(_roll_static)/slice | solution.py:107
  84.9 4.6 %fusion.57 = (f32[9,5,2,8,127]{0,3,4,2,1:T(8,128)}, f32[9,5,2,8,127]{0,3,4,2,1:T(8,128)}) fusion(f32[9,5,2,8,128]{0,3,4,2,1:T(8,128)S(1)} %bitcast.139), kind=kLoop, calls=%fused_computation.142 | loop fusion | bytes 1463040 | tf_op jit(solution)/shard_map/jit(_roll_static)/slice | solution.py:107
  101.0 3.2 copy.156
  111.0 0.8 dynamic-update-slice.1
  111.9 2.1 fusion.42
  114.0 2.7 copy.151
  116.7 3.3 copy.153
  120.0 14.6 %all-gather.4.cloned.1.call-done = f32[9,5,8,2048]{3,0,2,1:T(8,128)} async-done(((f32[9,5,8,128]{3,0,2,1:T(8,128)}), f32[9,5,8,2048]{3,0,2,1:T(8,128)}) %all-gather.4.cloned.1.call-update) | async-done | bytes 2949136 | tf_op jit(solution)/shard_map/all_gather | solution.py:193
  134.6 5.7 %constant_dynamic-update-slice_fusion.3 = f32[9,5,8,4096]{3,0,2,1:T(8,128)} fusion(f32[9,5,8,2048]{3,0,2,1:T(8,128)} %all-gather.4.cloned.1.call-done), kind=kLoop, calls=%fused_computation.110 | loop fusion | bytes 8192000
  140.3 3.0 constant_dynamic-update-slice_fusion.2
  143.3 20.9 %fusion.50 = (f32[1,5,8,4096]{3,0,2,1:T(1,128)}, f32[1,5,8,4096]{3,0,2,1:T(1,128)}, f32[1,5,8,4096]{3,0,2,1:T(1,128)}, f32[1,5,8,4096]{3,0,2,1:T(1,128)}, f32[1,...) fusion(f32[9,5,8,4096]{3,0,2,1:T(8,128)} %constant_dynamic-upda, ...), kind=kLoop, calls=%fused_computation.135 | loop fusion | bytes 11796480 | tf_op jit(solution)/shard_map/slice | solution.py:125
  164.2 0.9 dynamic-slice_bitcast_fusion.8
  165.1 1.6 dynamic-slice_bitcast_fusion
  166.7 1.6 dynamic-slice_bitcast_fusion.2
  168.3 1.6 dynamic-slice_bitcast_fusion.4
  169.9 1.6 dynamic-slice_bitcast_fusion.6
  171.4 1.8 stack.79
  173.3 0.8 subtract_bitcast_fusion
  174.0 3.3 copy.157
  177.3 35.9 %fusion.7 = f32[9,5,2,8,128]{0,3,4,2,1:T(8,128)} fusion(f32[9,5,2,8,128]{0,3,4,2,1:T(8,128)} %copy.156, f32[9,5,2,8,128]{0,3,4,2,1:T(8,128)} %copy-done.1, f32[9,5,2,3,128]{0,3,4,2,1:T(4,128)} %copy.153, f32[9,5,2,3,128]{0,3,4,2,1:T(4,128)S(1)} %copy.151, f32[9,5,2,8,1]{0,3,4,2,1:T(8,128)} %get-tuple-element.331, ...), kind=kLoop, calls=%fused_computation.21 | loop fusion | flops 3133440 | bytes 3796104 | tf_op jit(solution)/shard_map/add | solution.py:199
  213.2 3.4 copy.159
  217.8 63.2 %all-reduce.6 = (f32[11520]{0:T(1024)S(1)}, f32[16]{0:T(128)S(1)}, f32[720]{0:T(1024)S(1)}) all-reduce(f32[11520]{0:T(1024)S(1)} %dynamic-update-slice, f32[16]{0:T(128)S(1)} %dynamic-update-slice.1, f32[720]{0:T(1024)S(1)} %get-tuple-element.282), channel_id=2, replica_groups=mesh['pitch'=16,'radial'=8,'axial'=2] {'pitch'}, use_global_device_ids=true, to_apply=%add.2 | all-reduce | flops 12256 | bytes 98048
  281.1 20.6 %while.30 = (s32[]{:T(128)}, f32[720]{0:T(1024)S(1)}, s32[]{:T(128)}, f32[16,720]{1,0:T(8,128)S(1)}, f32[16,1]{0,1:T(1,128)S(1)}, /*index=5*/s32[]{:T(128)}, s32[]{:T(128)}) while((s32[]{:T(128)}, f32[720]{0:T(1024)S(1)}, s32[]{:T(128)}, f32[16,720]{1,0:T(8,128)S(1)}, f32[16,1]{0,1:T(1,128)S(1)}, /*index=5*/s32[]{:T(128)}, ...), condition=%wide.region_1.2_spmd.clone, body=%wide.region_0.1_spmd.clone.sunk | while | flops 2884 | bytes 14517 | solution.py:40
  281.7 0.7 add_select_fusion.4
  292.0 0.7 add_select_fusion.4
  293.3 0.7 add_select_fusion.4
  294.6 0.7 add_select_fusion.4
  302.8 59.9 %all-reduce.5 = (f32[11520]{0:T(1024)S(1)}, f32[720]{0:T(1024)S(1)}) all-reduce(f32[11520]{0:T(1024)S(1)} %dynamic-update-slice.2, f32[720]{0:T(1024)S(1)} %get-tuple-element.280), channel_id=3, replica_groups=mesh['pitch'=16,'radial'=8,'axial'=2] {'pitch'}, use_global_device_ids=true, to_apply=%add.4 | all-reduce | flops 12240 | bytes 97920
  362.9 20.7 %while.31 = (s32[]{:T(128)}, f32[720]{0:T(1024)S(1)}, s32[]{:T(128)}, f32[16,720]{1,0:T(8,128)S(1)}, f32[16,1]{0,1:T(1,128)S(1)}, /*index=5*/s32[]{:T(128)}, s32[]{:T(128)}, s32[]{:T(128)}, s32[]{:T(128)}) while((s32[]{:T(128)}, f32[720]{0:T(1024)S(1)}, s32[]{:T(128)}, f32[16,720]{1,0:T(8,128)S(1)}, f32[16,1]{0,1:T(1,128)S(1)}, ...), condition=%wide.region_4.5_spmd.clone, body=%wide.region_3.4_spmd.clone.sunk | while | flops 2888 | bytes 14579 | solution.py:40
  363.5 0.7 add_select_fusion.5
  383.6 0.9 add_multiply_fusion
  (161 shorter events, 42.9 us)
Async XLA Ops:
  7.2 127.5 %all-gather.4.cloned.1.call-start = ((), (), s32[]{:S(2)}) async-start(), calls=%async_computation | async-start | bytes 5570560 | tf_op jit(solution)/shard_map/all_gather | solution.py:193
  8.4 4.2 %copy-start.5 = (f32[9,4,2,8,128]{4,0,3,2,1:T(8,128)}, f32[9,4,2,8,128]{4,0,3,2,1:T(8,128)S(1)}, u32[]{:S(2)}) copy-start(f32[9,4,2,8,128]{4,0,3,2,1:T(8,128)S(1)} %copy.155) | copy-start | bytes 884740
  9.4 3.2 copy-start.8
  9.4 25.2 %collective-permute-start.4 = (f32[9,5,8,128]{3,0,2,1:T(8,128)S(1)}, f32[9,5,8,128]{3,0,2,1:T(8,128)}, u32[]{:S(2)}, u32[]{:S(2)}) collective-permute-start(f32[9,5,8,128]{3,0,2,1:T(8,128)S(1)} %bitcast.141), channel_id=1, source_target_pairs={{0,1},{1,0},{2,3},{3,2},{4,5},{5,4},{6,7},{7,6},{8,9},{9,8},{10,11... | collective-permute-start | bytes 552968 | tf_op jit(solution)/shard_map/ppermute | solution.py:44
  25.2 5.2 %copy-start.9 = (f32[9,2,8,128]{3,2,1,0:T(8,128)S(1)}, f32[9,2,8,128]{3,2,1,0:T(8,128)}, u32[]{:S(2)}) copy-start(f32[9,2,8,128]{3,2,1,0:T(8,128)} %param.12) | copy-start | bytes 221188
  25.2 5.2 %copy-start.10 = (f32[9,2,8,128]{3,2,1,0:T(8,128)S(1)}, f32[9,2,8,128]{3,2,1,0:T(8,128)}, u32[]{:S(2)}) copy-start(f32[9,2,8,128]{3,2,1,0:T(8,128)} %copy.146) | copy-start | bytes 221188
  34.7 3.5 copy-start
  38.2 10.7 %copy-start.3 = (f32[9,2,8,128]{0,2,3,1:T(8,128)S(1)}, f32[9,2,8,128]{0,2,3,1:T(8,128)}, u32[]{:S(2)}) copy-start(f32[9,2,8,128]{0,2,3,1:T(8,128)} %copy.148) | copy-start | bytes 221188
  38.2 10.7 %copy-start.4 = (f32[9,1,2,8,128]{0,3,4,2,1:T(8,128)S(1)}, f32[9,1,2,8,128]{0,3,4,2,1:T(8,128)}, u32[]{:S(2)}) copy-start(f32[9,1,2,8,128]{0,3,4,2,1:T(8,128)} %copy.164) | copy-start | bytes 221188
  42.9 69.0 %collective-permute-start = (f32[9,5,2,8,3]{0,3,4,2,1:T(8,128)}, f32[9,5,2,8,3]{0,3,4,2,1:T(8,128)}, u32[]{:S(2)}, u32[]{:S(2)}) collective-permute-start(f32[9,5,2,8,3]{0,3,4,2,1:T(8,128)} %get-tuple-element.322), channel_id=1, source_target_pairs={{0,16},{16,32},{32,48},{48,64},{64,80},{80,96},{96,112},{112,128},... | collective-permute-start | bytes 25928 | tf_op jit(solution)/shard_map/ppermute | solution.py:21
  44.8 67.1 %collective-permute-start.1 = (f32[9,5,2,8,3]{0,3,4,2,1:T(8,128)}, f32[9,5,2,8,3]{0,3,4,2,1:T(8,128)}, u32[]{:S(2)}, u32[]{:S(2)}) collective-permute-start(f32[9,5,2,8,3]{0,3,4,2,1:T(8,128)} %get-tuple-element.323), channel_id=1, source_target_pairs={{16,0},{32,16},{48,32},{64,48},{80,64},{96,80},{112,96},{128,112},... | collective-permute-start | bytes 25928 | tf_op jit(solution)/shard_map/ppermute | solution.py:22
  49.3 2.3 copy-start.1
  54.1 10.7 %copy-start.15 = (s32[9]{0:T(128)S(1)}, s32[9]{0:T(128)}, u32[]{:S(2)}) copy-start(s32[9]{0:T(128)} %param.14) | copy-start | bytes 112
  54.1 14.4 %copy-start.6 = (f32[9,4,2,8,128]{4,0,3,2,1:T(8,128)S(1)}, f32[9,4,2,8,128]{4,0,3,2,1:T(8,128)}, u32[]{:S(2)}) copy-start(f32[9,4,2,8,128]{4,0,3,2,1:T(8,128)} %copy-done.5) | copy-start | bytes 884740
  57.6 56.4 %collective-permute-start.2 = (f32[9,5,2,3,128]{4,2,3,1,0:T(2,128)}, f32[9,5,2,3,128]{4,2,3,1,0:T(2,128)}, u32[]{:S(2)}, u32[]{:S(2)}) collective-permute-start(f32[9,5,2,3,128]{4,2,3,1,0:T(2,128)} %copy.150), channel_id=1, source_target_pairs={{2,0},{4,2},{6,4},{8,6},{10,8},{12,10},{14,12},{3,1},{5,3},{7,5},{... | collective-permute-start | bytes 414728 | tf_op jit(solution)/shard_map/ppermute | solution.py:22
  61.8 54.9 %collective-permute-start.3 = (f32[9,5,2,3,128]{4,2,3,1,0:T(2,128)}, f32[9,5,2,3,128]{4,2,3,1,0:T(2,128)}, u32[]{:S(2)}, u32[]{:S(2)}) collective-permute-start(f32[9,5,2,3,128]{4,2,3,1,0:T(2,128)} %copy.152), channel_id=1, source_target_pairs={{0,2},{2,4},{4,6},{6,8},{8,10},{10,12},{12,14},{1,3},{3,5},{5,7},{... | collective-permute-start | bytes 414728 | tf_op jit(solution)/shard_map/ppermute | solution.py:21
  70.1 10.1 %slice-start = ((s8[5242880]{0:T(1024)(128)(4,1)}), s8[4194304]{0:T(1024)(128)(4,1)S(1)}, s32[]{:S(2)}) async-start(s8[5242880]{0:T(1024)(128)(4,1)} %bitcast.138), calls=%async_computation.1 | async-start | bytes 8388608
  71.4 8.8 %slice-start.1 = ((s8[5242880]{0:T(1024)(128)(4,1)}), s8[1048576]{0:T(1024)(128)(4,1)S(1)}, s32[]{:S(2)}) async-start(s8[5242880]{0:T(1024)(128)(4,1)} %bitcast.138), calls=%async_computation.2 | async-start | bytes 2097152
  89.5 20.3 %copy-start.17 = (u32[256]{0:T(256)S(1)}, u32[256]{0:T(256)}, u32[]{:S(2)}) copy-start(u32[256]{0:T(256)} %constant.161) | copy-start | bytes 3076
  134.6 5.7 %copy-start.2 = (f32[9,5,8,2048]{3,0,2,1:T(8,128)S(1)}, f32[9,5,8,2048]{3,0,2,1:T(8,128)}, u32[]{:S(2)}) copy-start(f32[9,5,8,2048]{3,0,2,1:T(8,128)} %all-gather.4.cloned.1.call-done) | copy-start | bytes 8847364
  143.3 34.0 %copy-start.11 = (f32[9,5,2,8,1]{0,3,4,2,1:T(8,128)S(1)}, f32[9,5,2,8,1]{0,3,4,2,1:T(8,128)}, u32[]{:S(2)}) copy-start(f32[9,5,2,8,1]{0,3,4,2,1:T(8,128)} %get-tuple-element.330) | copy-start | bytes 8644
  213.2 3.4 copy-start.12
  213.2 88.5 %copy-start.13 = (f32[128,128]{1,0:T(8,128)S(1)}, f32[128,128]{1,0:T(8,128)}, u32[]{:S(2)}) copy-start(f32[128,128]{1,0:T(8,128)} %constant.152.clone) | copy-start | bytes 196612
  213.2 88.5 %copy-start.16 = (f32[128]{0:T(128)S(1)}, f32[128]{0:T(128)}, u32[]{:S(2)}) copy-start(f32[128]{0:T(128)} %constant.153.clone) | copy-start | bytes 1540
  213.2 170.4 %copy-start.14 = (f32[128]{0:T(128)S(1)}, f32[128]{0:T(128)}, u32[]{:S(2)}) copy-start(f32[128]{0:T(128)} %constant.154.clone) | copy-start | bytes 1540
  216.6 167.9 %copy-start.7 = (f32[9,5,2,8,128]{4,3,2,1,0:T(8,128)}, f32[9,5,2,8,128]{4,3,2,1,0:T(8,128)S(1)}, u32[]{:S(2)}) copy-start(f32[9,5,2,8,128]{4,3,2,1,0:T(8,128)S(1)} %copy.159) | copy-start | bytes 1105924
Sparse Core Ops, SparseCore 0:
  34.8 99.7 all-gather.3
where the time goes:
time: 393 us; the launch traced here: 391 us
  local copies, waits for them, and re-layouts  128 us (33%)
  blocking collectives  123 us (31%)
  other arithmetic  77 us (20%)
  between operations  31.6 us (8%)
  waiting for transfers between devices  14.6 us (4%)
  starting transfers between devices  13.3 us (3%)
    unnamed x2, blocking collectives  123 us
    add x1, other arithmetic, local(): residual + penalty[:, :, None] * chosen[None, None, :, None, None]  35.9 us
    unnamed x58, local copies, waits for them, and re-layouts  23.9 us
    slice x5, local copies, waits for them, and re-layouts, pitch_derivative(): jnp.roll(along_pitch, reach, axis=4)  21.1 us
    slice x1, local copies, waits for them, and re-layouts, cut_rows(): joined[member]  20.9 us
    select_n x32, other arithmetic, hop(): return jax.tree.map(lambda a, b: jnp.where(reached, a, b), new, before)  20.8 us
    dynamic_slice x64, local copies, waits for them, and re-layouts, hop(): new = combine(before, jax.tree.map(lambda part: part[at], everything))  19.5 us
    all_gather x1, waiting for transfers between devices, local(): whole = lax.all_gather(facing, 'pitch', axis=3, tiled=True)  14.6 us
  transfers between devices with their start and end apart: 6, of which 1 were waited for; matrix products, arithmetic and copies ran while one was open for 20% of the time, Pallas kernels for 0%

commit v1 on v0

v1 whole, which is shorter than its diff:
```python
import math

import jax
import jax.numpy as jnp
import numpy as np
from jax import lax
from jax.experimental import pallas as pl
from jax.experimental.pallas import tpu as pltpu
from jax.sharding import PartitionSpec as P

COEFFS = (0.75, -0.15, 1.0 / 60.0)
GAMMA_LESS = 0.4
HIGHEST = lax.Precision.HIGHEST

INST = 9
VARS = 5
PLANES = 2
ROWS = 8
WIDTH = 128
RING = 16
PAIRS = INST * VARS
PIECE = 3
SLOTS = RING * PIECE
LANES = SLOTS * ROWS
SENT = 40


def spectral_weights():
    return [0.5 * (-1.0) ** k / math.sin(math.pi * k / INST) for k in range(1, INST // 2 + 1)]


def tables():
    extent = WIDTH * RING
    eps = float(extent * extent // 16)
    rho = 2.0 * eps / (1.0 + 2.0 * eps + math.sqrt(1.0 + 4.0 * eps))
    gain = rho / (eps * (1.0 - rho * rho))
    lam = rho**WIDTH
    closing = 1.0 / (1.0 - lam**RING)
    at = np.arange(WIDTH)
    reach = np.zeros((WIDTH, WIDTH + 6))
    for k, weight in enumerate(COEFFS, 1):
        reach[at, at - k + 3] += weight
        reach[at, at + k + 3] -= weight
    spots = np.arange(-3, WIDTH + 3)
    green = gain * rho ** np.abs(at[:, None] - at[None, :])
    wide = gain * rho ** np.abs(spots[:, None] - at[None, :])
    local = np.concatenate([reach[:, 3:-3], reach @ wide, green], axis=1)
    rise = rho ** (WIDTH - 1.0 - at)
    fall = rho ** (at + 0.0)
    kappa = sum(weight * (rho**k - rho**-k) for k, weight in enumerate(COEFFS, 1))
    pick = np.zeros((16, WIDTH))
    pick[0:3, 0:3] = np.eye(3)
    pick[3:6, WIDTH - 3 :] = np.eye(3)
    pick[6] = kappa * rise
    pick[7] = -kappa * fall
    pick[8 + 6] = rise
    pick[8 + 7] = fall
    side = np.zeros((24, 2 * WIDTH))
    for c in range(3):
        for m in range(3):
            if 1 <= 3 + m - c <= 3:
                w = -COEFFS[3 + m - c - 1]
                side[3 + c, m] += w
                side[3 + c, WIDTH:] += w * gain * (rho ** np.abs(at - m) - rho ** (at - m + 0.0))
            if c + 1 + m <= 3:
                w = COEFFS[c + m]
                spot = WIDTH - 1 - m
                side[8 + c, spot] += w
                side[8 + c, WIDTH:] += w * gain * (
                    rho ** np.abs(at - spot) - rho ** (spot - at + 0.0)
                )
    side[16, WIDTH:] = gain * rho ** (at + 1.0)
    side[17, WIDTH:] = gain * rho ** (WIDTH - at + 0.0)
    sums = np.zeros((WIDTH, WIDTH))
    sums[:, 0:RING] = rise[:, None]
    sums[:, RING : 2 * RING] = fall[:, None]
    ring = np.arange(RING)
    powers = np.zeros((RING, WIDTH))
    powers[:, 0:RING] = closing * lam ** ((ring[None, :] - ring[:, None] - 1) % RING)
    powers[:, RING : 2 * RING] = closing * lam ** ((ring[:, None] - ring[None, :] - 1) % RING)
    return [np.asarray(t, np.float32) for t in (local, pick, side, sums, powers)]


def field(density, moments, v, a):
    return density[:, a] if v == 0 else moments[:, v - 1, a]


def dot(a, b, contract):
    return lax.dot_general(
        a, b, (contract, ((), ())), precision=HIGHEST, preferred_element_type=jnp.float32
    )


def row_index(shape):
    return lax.broadcasted_iota(jnp.int32, shape, len(shape) - 2)


def pack_kernel(density, moments, facing, first, last):
    axial = lax.axis_index("axial")
    base = (1 - axial) * RING
    low = row_index((INST, ROWS, WIDTH)) < 4
    for v in range(VARS):
        one, two = field(density, moments, v, 0), field(density, moments, v, 1)
        edge = jnp.where(axial == 0, two, one)
        heads = jnp.where(low, one, pltpu.roll(two, 4, 1))
        tails = jnp.where(low, pltpu.roll(one, 4, 1), two)
        for n in range(INST):
            pair = n * VARS + v
            facing[base + pair // PIECE, pair % PIECE] = edge[n]
            first[pair] = heads[n]
            last[pair] = tails[n]
    zero = jnp.zeros((ROWS, WIDTH), jnp.float32)
    for pair in range(PAIRS, SLOTS):
        facing[base + pair // PIECE, pair % PIECE] = zero


def fluxes(d, ma, mr, mp, e, both):
    inverse = 1.0 / d
    pressure = GAMMA_LESS * (e - 0.5 * (ma * ma + mr * mr + mp * mp) * inverse)
    vr = mr * inverse
    total = e + pressure
    radial = (mr, ma * vr, mr * vr + pressure, mp * vr, total * vr)
    if not both:
        return radial
    wp = mp * inverse
    return (mp, ma * wp, mr * wp, mp * wp + pressure, total * wp), radial


def main_kernel(density, moments, above, below, local, pick, res, upd, cols, sums, flux, rest):
    axial = lax.axis_index("axial")
    radial = lax.axis_index("radial")
    shape = (INST, ROWS, WIDTH)
    row = row_index(shape)
    low = row < 4
    known = jnp.where(low, (radial < lax.axis_size("radial") - 1).astype(jnp.int32), (radial > 0).astype(jnp.int32)) > 0
    weights = spectral_weights()
    zero = jnp.zeros((ROWS, WIDTH), jnp.float32)
    for a in range(PLANES):
        fields = [field(density, moments, v, a) for v in range(VARS)]
        rims = []
        for v in range(VARS):
            up = jnp.stack([above[n * VARS + v] for n in range(INST)])
            down = jnp.stack([below[n * VARS + v] for n in range(INST)])
            if a == 0:
                rims.append(jnp.where(low, up, pltpu.roll(down, 4, 1)))
            else:
                rims.append(jnp.where(low, pltpu.roll(up, 4, 1), down))
        along_pitch, along_radial = fluxes(*fields, True)
        beyond = fluxes(*rims, False)
        mask = jnp.where(axial == 0, a == PLANES - 1, a == 0).astype(jnp.float32)
        for v in range(VARS):
            own, rim = along_radial[v], jnp.where(known, beyond[v], 0.0)
            total = -mask * fields[v]
            for k, weight in enumerate(COEFFS, 1):
                ahead = pltpu.roll(jnp.where(row >= k, own, rim), ROWS - k, 1)
                behind = pltpu.roll(jnp.where(row < ROWS - k, own, rim), k, 1)
                total = total + weight * (ahead - behind)
            f = fields[v]
            for k, weight in enumerate(weights, 1):
                back = jnp.concatenate([f[INST - k :], f[: INST - k]], axis=0)
                forth = jnp.concatenate([f[k:], f[:k]], axis=0)
                total = total + weight * (back - forth)
            for n in range(INST):
                at = (a * SLOTS + n * VARS + v) * ROWS
                rest[at : at + ROWS] = total[n]
                flux[at : at + ROWS] = along_pitch[v][n]
        for pair in range(PAIRS, SLOTS):
            at = (a * SLOTS + pair) * ROWS
            rest[at : at + ROWS] = zero
            flux[at : at + ROWS] = zero
    through = dot(flux[...], local[:, 0 : 2 * WIDTH], ((1,), (0,)))
    res[...] = rest[...] + through[:, 0:WIDTH]
    upd[...] = through[:, WIDTH:] + dot(rest[...], local[:, 2 * WIDTH :], ((1,), (0,)))
    edge = dot(pick[0:8], flux[...], ((1,), (1,)))
    cols[...] = edge
    sums[...] = edge + dot(pick[8:16], rest[...], ((1,), (1,)))


def align_kernel(shifts, whole, sums, weigh, powers, out, rolled):
    axial = lax.axis_index("axial")
    place = lax.axis_index("pitch")
    extent = WIDTH * RING
    base = (1 - axial) * RING
    lane = lax.broadcasted_iota(jnp.int32, (ROWS, WIDTH), 1)
    for j in range(PIECE):
        inst = jnp.minimum((place * PIECE + j) // VARS, INST - 1)
        shift = shifts[inst]
        offset = jnp.where(axial == 1, shift, (extent - shift) & (extent - 1))
        blocks, within = offset >> 7, offset & (WIDTH - 1)
        turned = pltpu.roll(whole[pl.ds(base, RING), j], within, 2)
        rolled[0:RING] = turned
        rolled[RING : 2 * RING] = turned
        for d in range(RING):
            here = rolled[RING + d - blocks]
            before = rolled[RING - 1 + d - blocks]
            at = d * SENT + j * ROWS
            out[at : at + ROWS] = jnp.where(lane < within, before, here)
    tall = PIECE * ROWS
    carried = jnp.zeros((tall, WIDTH), jnp.float32)
    for d in range(RING):
        block = out[d * SENT : d * SENT + tall]
        carried = carried + dot(block, weigh[...], ((1,), (0,))) * powers[d : d + 1]
    spread = powers[pl.ds(place, 1)]
    column = lax.broadcasted_iota(jnp.int32, (8, WIDTH), 1)
    line = row_index((8, WIDTH))
    extra = jnp.where(
        line == 0,
        jnp.where(column < RING, spread, 0.0),
        jnp.where((line == 1) & (column >= RING), spread, 0.0),
    )
    left = jnp.concatenate([carried, extra], axis=0)
    target = (1 - axial) * LANES + place * tall
    spots = lax.broadcasted_iota(jnp.int32, (tall, 2 * LANES), 1)
    select = (spots == target + row_index((tall, 2 * LANES))).astype(jnp.float32)
    totals = pltpu.roll(sums[...], 2, 0)
    right = jnp.concatenate([select, totals], axis=0)
    carries = dot(left, right, ((0,), (0,)))
    for t in range(6):
        at = slice(t * WIDTH, (t + 1) * WIDTH)
        out[pl.ds(tall + t, RING, SENT)] = carries[0:RING, at]
        out[pl.ds(tall + 6 + t, RING, SENT)] = carries[RING : 2 * RING, at]


def final_kernel(res, upd, got, left, right, local, side, residual, update):
    axial = lax.axis_index("axial")
    tall = PIECE * ROWS
    windows = got[:, 0:tall].reshape(LANES, WIDTH)
    smoothed = dot(windows, local[:, 2 * WIDTH :], ((1,), (0,)))
    carries = jnp.sum(got[:, tall:SENT], axis=0)
    line = row_index((8, WIDTH))
    for t in range(6):
        a, part = t // 3, t % 3
        at = slice(t * WIDTH, (t + 1) * WIDTH)
        pair = jnp.where(
            line == 0, carries[t : t + 1], jnp.where(line == 1, carries[6 + t : 7 + t], 0.0)
        )
        sides = jnp.concatenate([left[:, at], right[:, at], pair], axis=0)
        added = dot(sides, side[...], ((0,), (0,)))
        mine = axial == 1 - a
        here = slice(part * WIDTH, (part + 1) * WIDTH)
        r = res[at] + added[:, 0:WIDTH] + jnp.where(mine, windows[here], 0.0)
        u = upd[at] + added[:, WIDTH:] + jnp.where(mine, smoothed[here], 0.0)
        for j in range(16):
            pair_at = part * 16 + j
            if pair_at < PAIRS:
                n, v = pair_at // VARS, pair_at % VARS
                residual[n, v, a] = r[j * ROWS : (j + 1) * ROWS]
                update[n, v, a] = u[j * ROWS : (j + 1) * ROWS]


def call(kernel, outs, scratch=(), scalars=0, work=(0, 0), inputs=0):
    vmem = pl.BlockSpec(memory_space=pltpu.VMEM)
    smem = pl.BlockSpec(memory_space=pltpu.SMEM)
    return pl.pallas_call(
        kernel,
        out_shape=[jax.ShapeDtypeStruct(s, jnp.float32) for s in outs],
        in_specs=[smem] * scalars + [vmem] * inputs,
        out_specs=[vmem] * len(outs),
        scratch_shapes=[pltpu.VMEM(s, jnp.float32) for s in scratch],
        cost_estimate=pl.CostEstimate(flops=work[0], bytes_accessed=work[1], transcendentals=0),
    )


def local_step(density, moments, shifts):
    local, pick, side, weigh, powers = [jnp.asarray(t) for t in tables()]
    height = PLANES * LANES
    facing, first, last = call(
        pack_kernel,
        [(2 * RING, PIECE, ROWS, WIDTH), (PAIRS, ROWS, WIDTH), (PAIRS, ROWS, WIDTH)],
        inputs=2,
        work=(10**6, 10**6),
    )(density, moments)
    whole = lax.all_to_all(facing, ("axial", "pitch"), 0, 0)
    count_r = lax.axis_size("radial")
    up = [(i, i + 1) for i in range(count_r - 1)]
    down = [(j, i) for i, j in up]
    above = lax.ppermute(first, "radial", down)
    below = lax.ppermute(last, "radial", up)
    res, upd, cols, sums = call(
        main_kernel,
        [(height, WIDTH), (height, WIDTH), (8, height), (8, height)],
        scratch=[(height, WIDTH), (height, WIDTH)],
        inputs=6,
        work=(10**8, 2 * 10**6),
    )(density, moments, above, below, local, pick)
    ring = [(i, (i + 1) % RING) for i in range(RING)]
    back = [(j, i) for i, j in ring]
    left = lax.ppermute(cols, "pitch", ring)
    right = lax.ppermute(cols, "pitch", back)
    (send,) = call(
        align_kernel,
        [(RING * SENT, WIDTH)],
        scratch=[(2 * RING, ROWS, WIDTH)],
        scalars=1,
        inputs=4,
        work=(10**7, 10**6),
    )(shifts, whole, sums, weigh, powers)
    got = lax.all_to_all(send.reshape(RING, SENT, WIDTH), "pitch", 0, 0)
    shape = (INST, VARS, PLANES, ROWS, WIDTH)
    return tuple(
        call(final_kernel, [shape, shape], inputs=7, work=(10**7, 2 * 10**6))(
            res, upd, got, left, right, local, side
        )
    )


def solution(mesh):
    in_specs = (P(None, "axial", "radial", "pitch"), P(None, None, "axial", "radial", "pitch"), P())
    out_specs = (
        P(None, None, "axial", "radial", "pitch"),
        P(None, None, "axial", "radial", "pitch"),
    )
    return jax.shard_map(
        local_step, mesh=mesh, in_specs=in_specs, out_specs=out_specs, check_vma=False
    )
```

time: 393 us -> 55.2 us (0.14)
  local copies, waits for them, and re-layouts: 128 us -> 2.17 us
  blocking collectives: 123 us -> 0 us
  other arithmetic: 77 us -> 0 us
  between operations: 31.6 us -> 0.7 us
  starting transfers between devices: 13.3 us -> 27.2 us
  Pallas kernels: 0 us -> 12.5 us
    unnamed x2 -> x0, blocking collectives: 123 us -> none
    slice x13 -> x0, local copies, waits for them, and re-layouts: 55.6 us -> none  [the longest x5 21.1 us: pitch_derivative(): jnp.roll(along_pitch, reach, axis=4)]
    add x5 -> x0, other arithmetic: 40.4 us -> none  [the longest x1 35.9 us: local(): residual + penalty[:, :, None] * chosen[None, None, :, None, None]]
    unnamed x58 -> x18, local copies, waits for them, and re-layouts: 23.9 us -> 2.17 us
    select_n x34 -> x0, other arithmetic: 20.9 us -> none  [the longest x32 20.8 us: hop(): return jax.tree.map(lambda a, b: jnp.where(reached, a, b), new, before)]
    dynamic_slice x64 -> x0, local copies, waits for them, and re-layouts: 19.5 us -> none  [hop(): new = combine(before, jax.tree.map(lambda part: part[at], everything))]
    all_to_all x0 -> x2, starting transfers between devices: none -> 18.7 us  [the longest x1 11.4 us: local_step(): whole = lax.all_to_all(facing, ('axial', 'pitch'), 0, 0)]
    all_gather x1 -> x0, waiting for transfers between devices: 14.6 us -> none  [local(): whole = lax.all_gather(facing, 'pitch', axis=3, tiled=True)]
  transfers between devices with their start and end apart: 6 -> 6, of which waited for: 1 -> 6; matrix products, arithmetic and copies ran while one was open for 20% -> 0% of each run, Pallas kernels for 0% -> 8%
where the time goes in v1:
time: 55.2 us; the launch traced here: 54.7 us
  starting transfers between devices  27.2 us (49%)
  Pallas kernels  12.5 us (23%)
  waiting for transfers between devices  12.2 us (22%)
  local copies, waits for them, and re-layouts  2.17 us (4%)
  between operations  0.7 us (1%)
    all_to_all x1, starting transfers between devices, local_step(): whole = lax.all_to_all(facing, ('axial', 'pitch'), 0, 0)  11.4 us
    all_to_all x1, starting transfers between devices, local_step(): got = lax.all_to_all(send.reshape(RING, SENT, WIDTH), 'pitch', 0, 0)  7.3 us
    ppermute x1, waiting for transfers between devices, local_step(): right = lax.ppermute(cols, 'pitch', back)  5.04 us
    pallas_call x1, Pallas kernels, local_step(): call(main_kernel, [(height, WIDTH), (height, WIDTH), (8, height), (8, hei...  4.14 us
    ppermute x1, starting transfers between devices, local_step(): right = lax.ppermute(cols, 'pitch', back)  4.11 us
    ppermute x1, waiting for transfers between devices, local_step(): below = lax.ppermute(last, 'radial', up)  3.83 us
    pallas_call x1, Pallas kernels, local_step(): call(align_kernel, [(RING * SENT, WIDTH)], scratch=[(2 * RING, ROWS, WIDT...  3.3 us
    pallas_call x1, Pallas kernels, local_step(): call(final_kernel, [shape, shape], inputs=7, work=(10 ** 7, 2 * 10 ** 6))  3.16 us
  transfers between devices with their start and end apart: 6, of which 6 were waited for; matrix products, arithmetic and copies ran while one was open for 0% of the time, Pallas kernels for 8%

profile of v1, /device:TPU:8, one launch (start us, length us, event | category | flops | bytes accessed | tf_op | source)
XLA Modules:
  0.0 54.7 jit_solution(12893984582651662787)
XLA Ops:
  0.6 1.9 %shard_map.95 = (f32[32,3,8,128]{3,2,1,0:T(8,128)}, f32[45,8,128]{2,1,0:T(8,128)}, f32[45,8,128]{2,1,0:T(8,128)}) custom-call(f32[9,2,8,128]{3,2,1,0:T(8,128)} %density.3, f32[9,4,2,8,128]{4,3,2,1,0:T(8,128)} %moments.3), custom_call_target="tpu_custom_call" | custom-call | flops 1000000 | bytes 1000000 | tf_op jit(solution)/shard_map/pallas_call | solution.py:267
  2.5 0.0 copy-start.7
  2.5 0.0 copy-start.6
  2.5 11.4 %all-to-all-start = ((f32[32,3,8,128]{3,2,1,0:T(8,128)}), f32[32,3,8,128]{3,2,1,0:T(8,128)S(1)}, u32[]{:S(2)}, u32[]{:S(2)}) async-start(f32[32,3,8,128]{3,2,1,0:T(8,128)} %get-tuple-element.13), calls=%async_computation | async-start | bytes 786432 | tf_op jit(solution)/shard_map/all_to_all | solution.py:273
  14.0 0.0 copy-done.7
  14.0 1.9 %collective-permute-start = (f32[45,8,128]{2,1,0:T(8,128)S(1)}, f32[45,8,128]{2,1,0:T(8,128)S(1)}, u32[]{:S(2)}, u32[]{:S(2)}) collective-permute-start(f32[45,8,128]{2,1,0:T(8,128)S(1)} %copy-done.7), channel_id=1, source_target_pairs={{2,0},{4,2},{6,4},{8,6},{10,8},{12,10},{14,12},{3,1},{5,3},{7,5},{... | collective-permute-start | bytes 552968 | tf_op jit(solution)/shard_map/ppermute | solution.py:277
  15.9 0.0 copy-done.6
  15.9 2.4 %collective-permute-start.1 = (f32[45,8,128]{2,1,0:T(8,128)S(1)}, f32[45,8,128]{2,1,0:T(8,128)S(1)}, u32[]{:S(2)}, u32[]{:S(2)}) collective-permute-start(f32[45,8,128]{2,1,0:T(8,128)S(1)} %copy-done.6), channel_id=1, source_target_pairs={{0,2},{2,4},{4,6},{6,8},{8,10},{10,12},{12,14},{1,3},{3,5},{5,7},{... | collective-permute-start | bytes 552968 | tf_op jit(solution)/shard_map/ppermute | solution.py:278
  18.3 0.6 %collective-permute-done.above = f32[45,8,128]{2,1,0:T(8,128)S(1)} collective-permute-done((f32[45,8,128]{2,1,0:T(8,128)S(1)}, f32[45,8,128]{2,1,0:T(8,128)S(1)}, u32[]{:S(2)}, u32[]{:S(2)}) %collective-permute-start) | collective-permute-done | bytes 184352 | tf_op jit(solution)/shard_map/ppermute | solution.py:277
  19.0 0.0 copy-start.2
  19.0 3.8 %collective-permute-done.1.below = f32[45,8,128]{2,1,0:T(8,128)S(1)} collective-permute-done((f32[45,8,128]{2,1,0:T(8,128)S(1)}, f32[45,8,128]{2,1,0:T(8,128)S(1)}, u32[]{:S(2)}, u32[]{:S(2)}) %collective-permute-start.1) | collective-permute-done | bytes 184352 | tf_op jit(solution)/shard_map/ppermute | solution.py:278
  22.8 0.0 copy-done.2
  22.8 0.0 copy-start.3
  22.8 0.7 %copy-done.3 = f32[45,8,128]{2,1,0:T(8,128)} copy-done((f32[45,8,128]{2,1,0:T(8,128)}, f32[45,8,128]{2,1,0:T(8,128)S(1)}, u32[]{:S(2)}) %copy-start.3) | copy-done | bytes 184344
  23.5 4.1 %shard_map.96 = (f32[768,128]{1,0:T(8,128)}, f32[768,128]{1,0:T(8,128)}, f32[8,768]{1,0:T(8,128)}, f32[8,768]{1,0:T(8,128)}) custom-call(f32[9,2,8,128]{3,2,1,0:T(8,128)} %density.3, f32[9,4,2,8,128]{4,3,2,1,0:T(8,128)} %moments.3, f32[45,8,128]{2,1,0:T(8,128)} %copy-done.2, f32[45,8,128]{2,1,0:T(8,128)} %copy-done.3, f32[128,384]{1,0:T(8,128)} %constant.10.clone.local, ...), custom_call_target="tpu_custom_call" | custom-call | flops 100000000 | bytes 2000000 | tf_op jit(solution)/shard_map/pallas_call | solution.py:279
  27.6 0.8 %all-to-all-done.whole = f32[32,3,8,128]{3,2,1,0:T(8,128)S(1)} async-done(((f32[32,3,8,128]{3,2,1,0:T(8,128)}), f32[32,3,8,128]{3,2,1,0:T(8,128)S(1)}, u32[]{:S(2)}, u32[]{:S(2)}) %all-to-all-start) | async-done | bytes 393248 | tf_op jit(solution)/shard_map/all_to_all | solution.py:273
  28.4 0.0 copy-start
  28.4 0.8 %copy-done = f32[32,3,8,128]{3,2,1,0:T(8,128)} copy-done((f32[32,3,8,128]{3,2,1,0:T(8,128)}, f32[32,3,8,128]{3,2,1,0:T(8,128)S(1)}, u32[]{:S(2)}) %copy-start) | copy-done | bytes 393240
  29.2 3.3 %shard_map.97 = f32[640,128]{1,0:T(8,128)} custom-call(s32[9]{0:T(128)} %shifts.1, f32[32,3,8,128]{3,2,1,0:T(8,128)} %copy-done, f32[8,768]{1,0:T(8,128)} %get-tuple-element.14.sums, f32[128,128]{1,0:T(8,128)} %constant.13.clone.weigh, f32[16,128]{1,0:T(8,128)} %constant.14.clone.powers), custom_call_target="tpu_custom_call" | custom-call | flops 10000000 | bytes 1000000 | tf_op jit(solution)/shard_map/pallas_call | solution.py:290
  32.5 0.0 copy-start.8
  32.5 7.3 %all-to-all-start.1 = ((f32[16,40,128]{2,1,0:T(8,128)}), f32[16,40,128]{2,1,0:T(8,128)S(1)}, u32[]{:S(2)}, u32[]{:S(2)}) async-start(f32[16,40,128]{2,1,0:T(8,128)} %bitcast.1), calls=%async_computation.1 | async-start | bytes 655360 | tf_op jit(solution)/shard_map/all_to_all | solution.py:298
  39.8 0.0 copy-done.8
  39.8 4.1 %collective-permute-start.3 = (f32[8,768]{1,0:T(8,128)S(1)}, f32[8,768]{1,0:T(8,128)S(1)}, u32[]{:S(2)}, u32[]{:S(2)}) collective-permute-start(f32[8,768]{1,0:T(8,128)S(1)} %copy-done.8), channel_id=1, source_target_pairs={{16,0},{32,16},{48,32},{64,48},{80,64},{96,80},{112,96},{128,112},... | collective-permute-start | bytes 73736 | tf_op jit(solution)/shard_map/ppermute | solution.py:289
  43.9 0.0 collective-permute-start.2
  43.9 5.0 %collective-permute-done.3.right = f32[8,768]{1,0:T(8,128)S(1)} collective-permute-done((f32[8,768]{1,0:T(8,128)S(1)}, f32[8,768]{1,0:T(8,128)S(1)}, u32[]{:S(2)}, u32[]{:S(2)}) %collective-permute-start.3) | collective-permute-done | bytes 24608 | tf_op jit(solution)/shard_map/ppermute | solution.py:289
  49.0 0.0 copy-start.4
  49.0 1.8 %collective-permute-done.2.left = f32[8,768]{1,0:T(8,128)S(1)} collective-permute-done((f32[8,768]{1,0:T(8,128)S(1)}, f32[8,768]{1,0:T(8,128)S(1)}, u32[]{:S(2)}, u32[]{:S(2)}) %collective-permute-start.2) | collective-permute-done | bytes 24608 | tf_op jit(solution)/shard_map/ppermute | solution.py:288
  50.7 0.0 copy-start.5
  50.7 0.1 all-to-all-done.1.got
  50.8 0.0 copy-start.1
  50.8 0.0 copy-done.4
  50.8 0.5 copy-done.5
  51.3 0.2 copy-done.1
  51.6 3.2 %shard_map.98 = (f32[9,5,2,8,128]{4,3,2,1,0:T(8,128)}, f32[9,5,2,8,128]{4,3,2,1,0:T(8,128)}) custom-call(f32[768,128]{1,0:T(8,128)} %get-tuple-element.11.res, f32[768,128]{1,0:T(8,128)} %get-tuple-element.12.upd, f32[16,40,128]{2,1,0:T(8,128)} %copy-done.1, f32[8,768]{1,0:T(8,128)} %copy-done.5, f32[8,768]{1,0:T(8,128)} %copy-done.4, ...), custom_call_target="tpu_custom_call" | custom-call | flops 10000000 | bytes 2000000 | tf_op jit(solution)/shard_map/pallas_call | solution.py:301
Async XLA Ops:
  2.5 11.5 %copy-start.7 = (f32[45,8,128]{2,1,0:T(8,128)S(1)}, f32[45,8,128]{2,1,0:T(8,128)}, u32[]{:S(2)}) copy-start(f32[45,8,128]{2,1,0:T(8,128)} %get-tuple-element.9) | copy-start | bytes 552964
  2.5 13.4 %copy-start.6 = (f32[45,8,128]{2,1,0:T(8,128)S(1)}, f32[45,8,128]{2,1,0:T(8,128)}, u32[]{:S(2)}) copy-start(f32[45,8,128]{2,1,0:T(8,128)} %get-tuple-element.10) | copy-start | bytes 552964
  2.5 25.9 %all-to-all-start = ((f32[32,3,8,128]{3,2,1,0:T(8,128)}), f32[32,3,8,128]{3,2,1,0:T(8,128)S(1)}, u32[]{:S(2)}, u32[]{:S(2)}) async-start(f32[32,3,8,128]{3,2,1,0:T(8,128)} %get-tuple-element.13), calls=%async_computation | async-start | bytes 786432 | tf_op jit(solution)/shard_map/all_to_all | solution.py:273
  14.0 5.0 %collective-permute-start = (f32[45,8,128]{2,1,0:T(8,128)S(1)}, f32[45,8,128]{2,1,0:T(8,128)S(1)}, u32[]{:S(2)}, u32[]{:S(2)}) collective-permute-start(f32[45,8,128]{2,1,0:T(8,128)S(1)} %copy-done.7), channel_id=1, source_target_pairs={{2,0},{4,2},{6,4},{8,6},{10,8},{12,10},{14,12},{3,1},{5,3},{7,5},{... | collective-permute-start | bytes 552968 | tf_op jit(solution)/shard_map/ppermute | solution.py:277
  15.9 6.9 %collective-permute-start.1 = (f32[45,8,128]{2,1,0:T(8,128)S(1)}, f32[45,8,128]{2,1,0:T(8,128)S(1)}, u32[]{:S(2)}, u32[]{:S(2)}) collective-permute-start(f32[45,8,128]{2,1,0:T(8,128)S(1)} %copy-done.6), channel_id=1, source_target_pairs={{0,2},{2,4},{4,6},{6,8},{8,10},{10,12},{12,14},{1,3},{3,5},{5,7},{... | collective-permute-start | bytes 552968 | tf_op jit(solution)/shard_map/ppermute | solution.py:278
  19.0 3.8 %copy-start.2 = (f32[45,8,128]{2,1,0:T(8,128)}, f32[45,8,128]{2,1,0:T(8,128)S(1)}, u32[]{:S(2)}) copy-start(f32[45,8,128]{2,1,0:T(8,128)S(1)} %collective-permute-done.above) | copy-start | bytes 552964
  22.8 0.7 %copy-start.3 = (f32[45,8,128]{2,1,0:T(8,128)}, f32[45,8,128]{2,1,0:T(8,128)S(1)}, u32[]{:S(2)}) copy-start(f32[45,8,128]{2,1,0:T(8,128)S(1)} %collective-permute-done.1.below) | copy-start | bytes 552964
  28.4 0.8 %copy-start = (f32[32,3,8,128]{3,2,1,0:T(8,128)}, f32[32,3,8,128]{3,2,1,0:T(8,128)S(1)}, u32[]{:S(2)}) copy-start(f32[32,3,8,128]{3,2,1,0:T(8,128)S(1)} %all-to-all-done.whole) | copy-start | bytes 1179652
  32.5 7.3 %copy-start.8 = (f32[8,768]{1,0:T(8,128)S(1)}, f32[8,768]{1,0:T(8,128)}, u32[]{:S(2)}) copy-start(f32[8,768]{1,0:T(8,128)} %get-tuple-element.15) | copy-start | bytes 73732
  32.5 18.3 %all-to-all-start.1 = ((f32[16,40,128]{2,1,0:T(8,128)}), f32[16,40,128]{2,1,0:T(8,128)S(1)}, u32[]{:S(2)}, u32[]{:S(2)}) async-start(f32[16,40,128]{2,1,0:T(8,128)} %bitcast.1), calls=%async_computation.1 | async-start | bytes 655360 | tf_op jit(solution)/shard_map/all_to_all | solution.py:298
  39.8 9.2 %collective-permute-start.3 = (f32[8,768]{1,0:T(8,128)S(1)}, f32[8,768]{1,0:T(8,128)S(1)}, u32[]{:S(2)}, u32[]{:S(2)}) collective-permute-start(f32[8,768]{1,0:T(8,128)S(1)} %copy-done.8), channel_id=1, source_target_pairs={{16,0},{32,16},{48,32},{64,48},{80,64},{96,80},{112,96},{128,112},... | collective-permute-start | bytes 73736 | tf_op jit(solution)/shard_map/ppermute | solution.py:289
  43.9 6.8 %collective-permute-start.2 = (f32[8,768]{1,0:T(8,128)S(1)}, f32[8,768]{1,0:T(8,128)S(1)}, u32[]{:S(2)}, u32[]{:S(2)}) collective-permute-start(f32[8,768]{1,0:T(8,128)S(1)} %copy-done.8), channel_id=1, source_target_pairs={{0,16},{16,32},{32,48},{48,64},{64,80},{80,96},{96,112},{112,128},... | collective-permute-start | bytes 73736 | tf_op jit(solution)/shard_map/ppermute | solution.py:288
  49.0 1.9 %copy-start.4 = (f32[8,768]{1,0:T(8,128)}, f32[8,768]{1,0:T(8,128)S(1)}, u32[]{:S(2)}) copy-start(f32[8,768]{1,0:T(8,128)S(1)} %collective-permute-done.3.right) | copy-start | bytes 73732
  50.7 0.6 %copy-start.5 = (f32[8,768]{1,0:T(8,128)}, f32[8,768]{1,0:T(8,128)S(1)}, u32[]{:S(2)}) copy-start(f32[8,768]{1,0:T(8,128)S(1)} %collective-permute-done.2.left) | copy-start | bytes 73732
  50.8 0.7 %copy-start.1 = (f32[16,40,128]{2,1,0:T(8,128)}, f32[16,40,128]{2,1,0:T(8,128)S(1)}, u32[]{:S(2)}) copy-start(f32[16,40,128]{2,1,0:T(8,128)S(1)} %all-to-all-done.1.got) | copy-start | bytes 983044

commit v2 on v1

--- a/solution.py
+++ b/solution.py
@@ -7,6 +7,7 @@
 from jax.experimental import pallas as pl
 from jax.experimental.pallas import tpu as pltpu
 from jax.sharding import PartitionSpec as P
+
 
 COEFFS = (0.75, -0.15, 1.0 / 60.0)
 GAMMA_LESS = 0.4
@@ -23,6 +24,7 @@
 SLOTS = RING * PIECE
 LANES = SLOTS * ROWS
 SENT = 40
+GRANT = 16 * 2**20
 
 
 def spectral_weights():
@@ -95,38 +97,54 @@
     return lax.broadcasted_iota(jnp.int32, shape, len(shape) - 2)
 
 
-def pack_kernel(density, moments, facing, first, last):
-    axial = lax.axis_index("axial")
-    base = (1 - axial) * RING
+def edge_kernel(density, moments, facing, sems):
+    plane = 1 - lax.axis_index("axial")
+    copies = []
+    for v in range(VARS):
+        source = density.at[:, plane] if v == 0 else moments.at[:, v - 1, plane]
+        copies.append(
+            pltpu.make_async_copy(source, facing.at[pl.ds(v * INST, INST)], sems.at[v])
+        )
+    for copy in copies:
+        copy.start()
+    facing[PAIRS:SLOTS] = jnp.zeros((SLOTS - PAIRS, ROWS, WIDTH), jnp.float32)
+    for copy in copies:
+        copy.wait()
+
+
+def pack_kernel(density, moments, pick, first, last, cols, flux):
     low = row_index((INST, ROWS, WIDTH)) < 4
     for v in range(VARS):
         one, two = field(density, moments, v, 0), field(density, moments, v, 1)
-        edge = jnp.where(axial == 0, two, one)
-        heads = jnp.where(low, one, pltpu.roll(two, 4, 1))
-        tails = jnp.where(low, pltpu.roll(one, 4, 1), two)
-        for n in range(INST):
-            pair = n * VARS + v
-            facing[base + pair // PIECE, pair % PIECE] = edge[n]
-            first[pair] = heads[n]
-            last[pair] = tails[n]
-    zero = jnp.zeros((ROWS, WIDTH), jnp.float32)
-    for pair in range(PAIRS, SLOTS):
-        facing[base + pair // PIECE, pair % PIECE] = zero
-
-
-def fluxes(d, ma, mr, mp, e, both):
+        at = slice(v * INST, (v + 1) * INST)
+        first[at] = jnp.where(low, one, pltpu.roll(two, 4, 1))
+        last[at] = jnp.where(low, pltpu.roll(one, 4, 1), two)
+    for a in range(PLANES):
+        along = fluxes(*[field(density, moments, v, a) for v in range(VARS)], 2)
+        put(flux, a, along)
+    cols[...] = dot(pick[0:8], flux[...], ((1,), (1,)))
+
+
+def put(ref, a, values):
+    for v in range(VARS):
+        at = (a * SLOTS + v * INST) * ROWS
+        ref[at : at + INST * ROWS] = values[v].reshape(INST * ROWS, WIDTH)
+    at = (a * SLOTS + PAIRS) * ROWS
+    ref[at : (a + 1) * LANES] = jnp.zeros(((SLOTS - PAIRS) * ROWS, WIDTH), jnp.float32)
+
+
+def fluxes(d, ma, mr, mp, e, dim):
     inverse = 1.0 / d
     pressure = GAMMA_LESS * (e - 0.5 * (ma * ma + mr * mr + mp * mp) * inverse)
-    vr = mr * inverse
     total = e + pressure
-    radial = (mr, ma * vr, mr * vr + pressure, mp * vr, total * vr)
-    if not both:
-        return radial
-    wp = mp * inverse
-    return (mp, ma * wp, mr * wp, mp * wp + pressure, total * wp), radial
-
-
-def main_kernel(density, moments, above, below, local, pick, res, upd, cols, sums, flux, rest):
+    if dim == 1:
+        speed = mr * inverse
+        return (mr, ma * speed, mr * speed + pressure, mp * speed, total * speed)
+    speed = mp * inverse
+    return (mp, ma * speed, mr * speed, mp * speed + pressure, total * speed)
+
+
+def main_kernel(density, moments, above, below, local, pick, res, upd, sums, flux, rest):
     axial = lax.axis_index("axial")
     radial = lax.axis_index("radial")
     shape = (INST, ROWS, WIDTH)
@@ -134,19 +152,19 @@
     low = row < 4
     known = jnp.where(low, (radial < lax.axis_size("radial") - 1).astype(jnp.int32), (radial > 0).astype(jnp.int32)) > 0
     weights = spectral_weights()
-    zero = jnp.zeros((ROWS, WIDTH), jnp.float32)
     for a in range(PLANES):
         fields = [field(density, moments, v, a) for v in range(VARS)]
         rims = []
         for v in range(VARS):
-            up = jnp.stack([above[n * VARS + v] for n in range(INST)])
-            down = jnp.stack([below[n * VARS + v] for n in range(INST)])
+            at = slice(v * INST, (v + 1) * INST)
+            up, down = above[at], below[at]
             if a == 0:
                 rims.append(jnp.where(low, up, pltpu.roll(down, 4, 1)))
             else:
                 rims.append(jnp.where(low, pltpu.roll(up, 4, 1), down))
-        along_pitch, along_radial = fluxes(*fields, True)
-        beyond = fluxes(*rims, False)
+        along_radial, beyond = fluxes(*fields, 1), fluxes(*rims, 1)
+        put(flux, a, fluxes(*fields, 2))
+        added = []
         mask = jnp.where(axial == 0, a == PLANES - 1, a == 0).astype(jnp.float32)
         for v in range(VARS):
             own, rim = along_radial[v], jnp.where(known, beyond[v], 0.0)
@@ -160,46 +178,42 @@
                 back = jnp.concatenate([f[INST - k :], f[: INST - k]], axis=0)
                 forth = jnp.concatenate([f[k:], f[:k]], axis=0)
                 total = total + weight * (back - forth)
-            for n in range(INST):
-                at = (a * SLOTS + n * VARS + v) * ROWS
-                rest[at : at + ROWS] = total[n]
-                flux[at : at + ROWS] = along_pitch[v][n]
-        for pair in range(PAIRS, SLOTS):
-            at = (a * SLOTS + pair) * ROWS
-            rest[at : at + ROWS] = zero
-            flux[at : at + ROWS] = zero
+            added.append(total)
+        put(rest, a, added)
     through = dot(flux[...], local[:, 0 : 2 * WIDTH], ((1,), (0,)))
     res[...] = rest[...] + through[:, 0:WIDTH]
     upd[...] = through[:, WIDTH:] + dot(rest[...], local[:, 2 * WIDTH :], ((1,), (0,)))
-    edge = dot(pick[0:8], flux[...], ((1,), (1,)))
-    cols[...] = edge
-    sums[...] = edge + dot(pick[8:16], rest[...], ((1,), (1,)))
-
-
-def align_kernel(shifts, whole, sums, weigh, powers, out, rolled):
+    sums[...] = dot(pick[0:8], flux[...], ((1,), (1,))) + dot(
+        pick[8:16], rest[...], ((1,), (1,))
+    )
+
+
+def align_kernel(shifts, whole, sums, weigh, powers, out, rolled, kept):
     axial = lax.axis_index("axial")
     place = lax.axis_index("pitch")
     extent = WIDTH * RING
-    base = (1 - axial) * RING
+    tall = PIECE * ROWS
     lane = lax.broadcasted_iota(jnp.int32, (ROWS, WIDTH), 1)
     for j in range(PIECE):
-        inst = jnp.minimum((place * PIECE + j) // VARS, INST - 1)
+        inst = lax.rem(place * PIECE + j, INST)
         shift = shifts[inst]
         offset = jnp.where(axial == 1, shift, (extent - shift) & (extent - 1))
         blocks, within = offset >> 7, offset & (WIDTH - 1)
-        turned = pltpu.roll(whole[pl.ds(base, RING), j], within, 2)
+        turned = pltpu.roll(whole[:, j], within, 2)
         rolled[0:RING] = turned
         rolled[RING : 2 * RING] = turned
         for d in range(RING):
             here = rolled[RING + d - blocks]
             before = rolled[RING - 1 + d - blocks]
+            window = jnp.where(lane < within, before, here)
             at = d * SENT + j * ROWS
-            out[at : at + ROWS] = jnp.where(lane < within, before, here)
-    tall = PIECE * ROWS
-    carried = jnp.zeros((tall, WIDTH), jnp.float32)
-    for d in range(RING):
-        block = out[d * SENT : d * SENT + tall]
-        carried = carried + dot(block, weigh[...], ((1,), (0,))) * powers[d : d + 1]
+            out[at : at + ROWS] = window
+            at = d * tall + j * ROWS
+            kept[at : at + ROWS] = window
+    totals = dot(kept[...], weigh[...], ((1,), (0,)))
+    carried = totals[0:tall] * powers[0:1]
+    for d in range(1, RING):
+        carried = carried + totals[d * tall : (d + 1) * tall] * powers[d : d + 1]
     spread = powers[pl.ds(place, 1)]
     column = lax.broadcasted_iota(jnp.int32, (8, WIDTH), 1)
     line = row_index((8, WIDTH))
@@ -212,8 +226,7 @@
     target = (1 - axial) * LANES + place * tall
     spots = lax.broadcasted_iota(jnp.int32, (tall, 2 * LANES), 1)
     select = (spots == target + row_index((tall, 2 * LANES))).astype(jnp.float32)
-    totals = pltpu.roll(sums[...], 2, 0)
-    right = jnp.concatenate([select, totals], axis=0)
+    right = jnp.concatenate([select, pltpu.roll(sums[...], 2, 0)], axis=0)
     carries = dot(left, right, ((0,), (0,)))
     for t in range(6):
         at = slice(t * WIDTH, (t + 1) * WIDTH)
@@ -221,13 +234,14 @@
         out[pl.ds(tall + 6 + t, RING, SENT)] = carries[RING : 2 * RING, at]
 
 
-def final_kernel(res, upd, got, left, right, local, side, residual, update):
+def final_kernel(res, upd, got, left, right, local, side, residual, update, first, second, sems):
     axial = lax.axis_index("axial")
     tall = PIECE * ROWS
     windows = got[:, 0:tall].reshape(LANES, WIDTH)
     smoothed = dot(windows, local[:, 2 * WIDTH :], ((1,), (0,)))
     carries = jnp.sum(got[:, tall:SENT], axis=0)
     line = row_index((8, WIDTH))
+    copies = []
     for t in range(6):
         a, part = t // 3, t % 3
         at = slice(t * WIDTH, (t + 1) * WIDTH)
@@ -243,9 +257,16 @@
         for j in range(16):
             pair_at = part * 16 + j
             if pair_at < PAIRS:
-                n, v = pair_at // VARS, pair_at % VARS
-                residual[n, v, a] = r[j * ROWS : (j + 1) * ROWS]
-                update[n, v, a] = u[j * ROWS : (j + 1) * ROWS]
+                v, n = pair_at // INST, pair_at % INST
+                first[a, n, v] = r[j * ROWS : (j + 1) * ROWS]
+                second[a, n, v] = u[j * ROWS : (j + 1) * ROWS]
+        if part == 2:
+            for i, (held, out) in enumerate(((first, residual), (second, update))):
+                copy = pltpu.make_async_copy(held.at[a], out.at[:, :, a], sems.at[2 * a + i])
+                copy.start()
+                copies.append(copy)
+    for copy in copies:
+        copy.wait()
 
 
 def call(kernel, outs, scratch=(), scalars=0, work=(0, 0), inputs=0):
@@ -258,50 +279,66 @@
         out_specs=[vmem] * len(outs),
         scratch_shapes=[pltpu.VMEM(s, jnp.float32) for s in scratch],
         cost_estimate=pl.CostEstimate(flops=work[0], bytes_accessed=work[1], transcendentals=0),
+        compiler_params=pltpu.CompilerParams(vmem_limit_bytes=GRANT),
     )
 
 
 def local_step(density, moments, shifts):
     local, pick, side, weigh, powers = [jnp.asarray(t) for t in tables()]
     height = PLANES * LANES
-    facing, first, last = call(
+    facing = pl.pallas_call(
+        edge_kernel,
+        out_shape=jax.ShapeDtypeStruct((SLOTS, ROWS, WIDTH), jnp.float32),
+        in_specs=[pl.BlockSpec(memory_space=pl.ANY)] * 2,
+        out_specs=pl.BlockSpec(memory_space=pltpu.VMEM),
+        scratch_shapes=[pltpu.SemaphoreType.DMA((VARS,))],
+    )(density, moments)
+    across = lax.ppermute(facing, "axial", [(0, 1), (1, 0)])
+    first, last, cols = call(
         pack_kernel,
-        [(2 * RING, PIECE, ROWS, WIDTH), (PAIRS, ROWS, WIDTH), (PAIRS, ROWS, WIDTH)],
-        inputs=2,
+        [(PAIRS, ROWS, WIDTH), (PAIRS, ROWS, WIDTH), (8, height)],
+        scratch=[(height, WIDTH)],
+        inputs=3,
         work=(10**6, 10**6),
-    )(density, moments)
-    whole = lax.all_to_all(facing, ("axial", "pitch"), 0, 0)
+    )(density, moments, pick)
     count_r = lax.axis_size("radial")
     up = [(i, i + 1) for i in range(count_r - 1)]
     down = [(j, i) for i, j in up]
     above = lax.ppermute(first, "radial", down)
     below = lax.ppermute(last, "radial", up)
-    res, upd, cols, sums = call(
+    ring = [(i, (i + 1) % RING) for i in range(RING)]
+    back = [(j, i) for i, j in ring]
+    left = lax.ppermute(cols, "pitch", ring)
+    right = lax.ppermute(cols, "pitch", back)
+    whole = lax.all_to_all(across.reshape(RING, PIECE, ROWS, WIDTH), "pitch", 0, 0)
+    res, upd, sums = call(
         main_kernel,
-        [(height, WIDTH), (height, WIDTH), (8, height), (8, height)],
+        [(height, WIDTH), (height, WIDTH), (8, height)],
         scratch=[(height, WIDTH), (height, WIDTH)],
         inputs=6,
         work=(10**8, 2 * 10**6),
     )(density, moments, above, below, local, pick)
-    ring = [(i, (i + 1) % RING) for i in range(RING)]
-    back = [(j, i) for i, j in ring]
-    left = lax.ppermute(cols, "pitch", ring)
-    right = lax.ppermute(cols, "pitch", back)
     (send,) = call(
         align_kernel,
         [(RING * SENT, WIDTH)],
-        scratch=[(2 * RING, ROWS, WIDTH)],
+        scratch=[(2 * RING, ROWS, WIDTH), (RING * PIECE * ROWS, WIDTH)],
         scalars=1,
         inputs=4,
         work=(10**7, 10**6),
     )(shifts, whole, sums, weigh, powers)
+    send, left, right = lax.optimization_barrier((send, left, right))
     got = lax.all_to_all(send.reshape(RING, SENT, WIDTH), "pitch", 0, 0)
     shape = (INST, VARS, PLANES, ROWS, WIDTH)
-    return tuple(
-        call(final_kernel, [shape, shape], inputs=7, work=(10**7, 2 * 10**6))(
-            res, upd, got, left, right, local, side
-        )
-    )
+    held = pltpu.VMEM((PLANES, INST, VARS, ROWS, WIDTH), jnp.float32)
+    return pl.pallas_call(
+        final_kernel,
+        out_shape=[jax.ShapeDtypeStruct(shape, jnp.float32)] * 2,
+        in_specs=[pl.BlockSpec(memory_space=pltpu.VMEM)] * 7,
+        out_specs=[pl.BlockSpec(memory_space=pl.ANY)] * 2,
+        scratch_shapes=[held, held, pltpu.SemaphoreType.DMA((2 * PLANES,))],
+        cost_estimate=pl.CostEstimate(flops=10**7, bytes_accessed=2 * 10**6, transcendentals=0),
+        compiler_params=pltpu.CompilerParams(vmem_limit_bytes=GRANT),
+    )(res, upd, got, left, right, local, side)
 
 
 def solution(mesh):

time: 55.2 us -> 55.6 us (level)
  blocking collectives: 0 us -> 17.4 us
  starting transfers between devices: 27.2 us -> 21.2 us
  waiting for transfers between devices: 12.2 us -> 6.91 us
  Pallas kernels: 12.5 us -> 7.84 us
  local copies, waits for them, and re-layouts: 2.17 us -> 0.67 us
    all_to_all x0 -> x1, blocking collectives: none -> 17.4 us  [local_step(): got = lax.all_to_all(send.reshape(RING, SENT, WIDTH), 'pitch', 0, 0)]
    all_to_all x2 -> x1, starting transfers between devices: 18.7 us -> 9.63 us  [local_step(): lax.all_to_all(across.reshape(RING, PIECE, ROWS, WIDTH), 'pitch', 0, 0)]
    ppermute x0 -> x1, waiting for transfers between devices: none -> 5.44 us  [local_step(): across = lax.ppermute(facing, 'axial', [(0, 1), (1, 0)])]
    ppermute x1, waiting for transfers between devices: 5.04 us -> 0.01 us  [local_step(): right = lax.ppermute(cols, 'pitch', back)]
    ppermute x1, waiting for transfers between devices: 3.83 us -> 0.3 us  [local_step(): below = lax.ppermute(last, 'radial', up)]
    ppermute x0 -> x1, starting transfers between devices: none -> 3.11 us  [local_step(): across = lax.ppermute(facing, 'axial', [(0, 1), (1, 0)])]
    pallas_call x3 -> x4, Pallas kernels: 9.2 us -> 6.16 us  [the longest x1 2.31 us: local_step(): call(main_kernel, [(height, WIDTH), (height, WIDTH), (8, height)], scratc...]
    pallas_call x1, Pallas kernels: 3.3 us -> 1.68 us  [local_step(): call(align_kernel, [(RING * SENT, WIDTH)], scratch=[(2 * RING, ROWS, WIDT...]
  transfers between devices with their start and end apart: 6 -> 6, of which waited for: 6 -> 3; matrix products, arithmetic and copies ran while one was open for 0% -> 0% of each run, Pallas kernels for 8% -> 8%
where the time goes in v2:
time: 55.6 us; the launch traced here: 54.8 us
  starting transfers between devices  21.2 us (38%)
  blocking collectives  17.4 us (31%)
  Pallas kernels  7.84 us (14%)
  waiting for transfers between devices  6.91 us (12%)
  between operations  0.76 us (1%)
  local copies, waits for them, and re-layouts  0.67 us (1%)
    all_to_all x1, blocking collectives, local_step(): got = lax.all_to_all(send.reshape(RING, SENT, WIDTH), 'pitch', 0, 0)  17.4 us
    all_to_all x1, starting transfers between devices, local_step(): lax.all_to_all(across.reshape(RING, PIECE, ROWS, WIDTH), 'pitch', 0, 0)  9.63 us
    ppermute x1, waiting for transfers between devices, local_step(): across = lax.ppermute(facing, 'axial', [(0, 1), (1, 0)])  5.44 us
    ppermute x1, starting transfers between devices, local_step(): right = lax.ppermute(cols, 'pitch', back)  4.11 us
    ppermute x1, starting transfers between devices, local_step(): across = lax.ppermute(facing, 'axial', [(0, 1), (1, 0)])  3.11 us
    ppermute x1, starting transfers between devices, local_step(): below = lax.ppermute(last, 'radial', up)  2.41 us
    pallas_call x1, Pallas kernels, local_step(): call(main_kernel, [(height, WIDTH), (height, WIDTH), (8, height)], scratc...  2.31 us
    ppermute x1, starting transfers between devices, local_step(): above = lax.ppermute(first, 'radial', down)  1.93 us
  transfers between devices with their start and end apart: 6, of which 3 were waited for; matrix products, arithmetic and copies ran while one was open for 0% of the time, Pallas kernels for 8%

profile of v2, /device:TPU:8, one launch (start us, length us, event | category | flops | bytes accessed | tf_op | source)
XLA Modules:
  0.0 54.8 jit_solution(15183337019683564267)
XLA Ops:
  0.6 1.6 %shard_map.97 = f32[48,8,128]{2,1,0:T(8,128)} custom-call(f32[9,2,8,128]{3,2,1,0:T(8,128)} %density.5, f32[9,4,2,8,128]{4,3,2,1,0:T(8,128)} %moments.5), custom_call_target="tpu_custom_call" | custom-call | tf_op jit(solution)/shard_map/pallas_call | solution.py:289
  2.2 0.0 copy-start
  2.2 3.1 %collective-permute-start.2 = (f32[48,8,128]{2,1,0:T(8,128)}, f32[48,8,128]{2,1,0:T(8,128)}, u32[]{:S(2)}, u32[]{:S(2)}) collective-permute-start(f32[48,8,128]{2,1,0:T(8,128)} %shard_map.97), channel_id=1, source_target_pairs={{0,1},{1,0},{2,3},{3,2},{4,5},{5,4},{6,7},{7,6},{8,9},{9,8},{10,11... | collective-permute-start | bytes 589832 | tf_op jit(solution)/shard_map/ppermute | solution.py:296
  5.3 5.4 %collective-permute-done.2 = f32[48,8,128]{2,1,0:T(8,128)} collective-permute-done((f32[48,8,128]{2,1,0:T(8,128)}, f32[48,8,128]{2,1,0:T(8,128)}, u32[]{:S(2)}, u32[]{:S(2)}) %collective-permute-start.2) | collective-permute-done | bytes 196640 | tf_op jit(solution)/shard_map/ppermute | solution.py:296
  10.8 0.0 copy-start.2
  10.8 0.0 copy-start.4
  10.8 9.6 %all-to-all-start = ((f32[16,3,8,128]{3,2,1,0:T(8,128)}), f32[16,3,8,128]{3,2,1,0:T(8,128)S(1)}, u32[]{:S(2)}, u32[]{:S(2)}) async-start(f32[16,3,8,128]{3,2,1,0:T(8,128)} %bitcast), calls=%async_computation | async-start | bytes 393216 | tf_op jit(solution)/shard_map/all_to_all | solution.py:313
  20.4 0.0 copy-done
  20.4 0.0 copy-done.2
  20.4 0.0 copy-done.4
  20.4 0.0 copy-start.1
  20.4 0.5 shard_map.95
  21.0 1.9 %collective-permute-start = (f32[45,8,128]{2,1,0:T(8,128)S(1)}, f32[45,8,128]{2,1,0:T(8,128)S(1)}, u32[]{:S(2)}, u32[]{:S(2)}) collective-permute-start(f32[45,8,128]{2,1,0:T(8,128)S(1)} %get-tuple-element.11), channel_id=1, source_target_pairs={{2,0},{4,2},{6,4},{8,6},{10,8},{12,10},{14,12},{3,1},{5,3},{7,5},{... | collective-permute-start | bytes 552968 | tf_op jit(solution)/shard_map/ppermute | solution.py:307
  22.9 2.4 %collective-permute-start.1 = (f32[45,8,128]{2,1,0:T(8,128)S(1)}, f32[45,8,128]{2,1,0:T(8,128)S(1)}, u32[]{:S(2)}, u32[]{:S(2)}) collective-permute-start(f32[45,8,128]{2,1,0:T(8,128)S(1)} %get-tuple-element.12), channel_id=1, source_target_pairs={{0,2},{2,4},{4,6},{6,8},{8,10},{10,12},{12,14},{1,3},{3,5},{5,7},{... | collective-permute-start | bytes 552968 | tf_op jit(solution)/shard_map/ppermute | solution.py:308
  25.3 0.0 copy-start.3
  25.3 0.0 copy-start.6
  25.4 4.1 %collective-permute-start.4 = (f32[8,768]{1,0:T(8,128)S(1)}, f32[8,768]{1,0:T(8,128)S(1)}, u32[]{:S(2)}, u32[]{:S(2)}) collective-permute-start(f32[8,768]{1,0:T(8,128)S(1)} %get-tuple-element.16), channel_id=1, source_target_pairs={{16,0},{32,16},{48,32},{64,48},{80,64},{96,80},{112,96},{128,112},... | collective-permute-start | bytes 73736 | tf_op jit(solution)/shard_map/ppermute | solution.py:312
  29.5 0.0 collective-permute-start.3
  29.5 0.0 collective-permute-done.above
  29.5 0.3 collective-permute-done.1.below
  29.8 0.0 copy-done.1
  29.8 2.3 %shard_map.96 = (f32[768,128]{1,0:T(8,128)S(1)}, f32[768,128]{1,0:T(8,128)S(1)}, f32[8,768]{1,0:T(8,128)S(1)}) custom-call(f32[9,2,8,128]{3,2,1,0:T(8,128)S(1)} %copy-done.2, f32[9,4,2,8,128]{4,3,2,1,0:T(8,128)S(1)} %copy-done, f32[45,8,128]{2,1,0:T(8,128)S(1)} %collective-permute-done.above, f32[45,8,128]{2,1,0:T(8,128)S(1)} %collective-permute-done.1.below, ...), custom_call_target="tpu_custom_call" | custom-call | flops 100000000 | bytes 2000000 | tf_op jit(solution)/shard_map/pallas_call | solution.py:314
  32.1 0.0 copy-start.7
  32.1 0.0 all-to-all-done.whole
  32.1 0.0 copy-done.3
  32.1 0.0 copy-done.6
  32.1 0.6 %copy-done.7 = s32[9]{0:T(128)S(1)} copy-done((s32[9]{0:T(128)S(1)}, s32[9]{0:T(128)}, u32[]{:S(2)}) %copy-start.7) | copy-done | bytes 60
  32.7 1.7 %shard_map.98 = f32[640,128]{1,0:T(8,128)S(1)} custom-call(s32[9]{0:T(128)S(1)} %copy-done.7, f32[16,3,8,128]{3,2,1,0:T(8,128)S(1)} %all-to-all-done.whole, f32[8,768]{1,0:T(8,128)S(1)} %get-tuple-element.15.sums, f32[128,128]{1,0:T(8,128)S(1)} %copy-done.3, f32[16,128]{1,0:T(8,128)S(1)} %copy-done.6), custom_call_target="tpu_custom_call" | custom-call | flops 10000000 | bytes 1000000 | tf_op jit(solution)/shard_map/pallas_call | solution.py:321
  34.4 0.0 collective-permute-done.4.right
  34.5 1.2 %collective-permute-done.3.left = f32[8,768]{1,0:T(8,128)S(1)} collective-permute-done((f32[8,768]{1,0:T(8,128)S(1)}, f32[8,768]{1,0:T(8,128)S(1)}, u32[]{:S(2)}, u32[]{:S(2)}) %collective-permute-start.3) | collective-permute-done | bytes 24608 | tf_op jit(solution)/shard_map/ppermute | solution.py:311
  35.6 0.0 copy-start.5
  35.6 17.4 %all_to_all.10.got = f32[16,40,128]{2,1,0:T(8,128)S(1)} all-to-all(f32[16,40,128]{2,1,0:T(8,128)S(1)} %bitcast.2), channel_id=1, replica_groups=mesh['pitch'=16,'radial'=8,'axial'=2] {'pitch'}, dimensions={0} | all-to-all | bytes 655360 | tf_op jit(solution)/shard_map/all_to_all | solution.py:330
  53.0 0.0 copy-done.5
  53.1 1.8 %shard_map.99 = (f32[9,5,2,8,128]{4,3,2,1,0:T(8,128)}, f32[9,5,2,8,128]{4,3,2,1,0:T(8,128)}) custom-call(f32[768,128]{1,0:T(8,128)S(1)} %get-tuple-element.13.res, f32[768,128]{1,0:T(8,128)S(1)} %get-tuple-element.14.upd, f32[16,40,128]{2,1,0:T(8,128)S(1)} %all_to_all.10.got, f32[8,768]{1,0:T(8,128)S(1)} %collective-permute-done.3.left, ...), custom_call_target="tpu_custom_call" | custom-call | flops 10000000 | bytes 2000000 | tf_op jit(solution)/shard_map/pallas_call | solution.py:333
Async XLA Ops:
  2.2 18.2 %copy-start = (f32[9,4,2,8,128]{4,3,2,1,0:T(8,128)S(1)}, f32[9,4,2,8,128]{4,3,2,1,0:T(8,128)}, u32[]{:S(2)}) copy-start(f32[9,4,2,8,128]{4,3,2,1,0:T(8,128)} %moments.5) | copy-start | bytes 884740
  2.2 8.5 %collective-permute-start.2 = (f32[48,8,128]{2,1,0:T(8,128)}, f32[48,8,128]{2,1,0:T(8,128)}, u32[]{:S(2)}, u32[]{:S(2)}) collective-permute-start(f32[48,8,128]{2,1,0:T(8,128)} %shard_map.97), channel_id=1, source_target_pairs={{0,1},{1,0},{2,3},{3,2},{4,5},{5,4},{6,7},{7,6},{8,9},{9,8},{10,11... | collective-permute-start | bytes 589832 | tf_op jit(solution)/shard_map/ppermute | solution.py:296
  10.8 9.7 %copy-start.2 = (f32[9,2,8,128]{3,2,1,0:T(8,128)S(1)}, f32[9,2,8,128]{3,2,1,0:T(8,128)}, u32[]{:S(2)}) copy-start(f32[9,2,8,128]{3,2,1,0:T(8,128)} %density.5) | copy-start | bytes 221188
  10.8 9.7 %copy-start.4 = (f32[16,128]{1,0:T(8,128)S(1)}, f32[16,128]{1,0:T(8,128)}, u32[]{:S(2)}) copy-start(f32[16,128]{1,0:T(8,128)} %constant.11.clone.pick) | copy-start | bytes 24580
  10.8 21.3 %all-to-all-start = ((f32[16,3,8,128]{3,2,1,0:T(8,128)}), f32[16,3,8,128]{3,2,1,0:T(8,128)S(1)}, u32[]{:S(2)}, u32[]{:S(2)}) async-start(f32[16,3,8,128]{3,2,1,0:T(8,128)} %bitcast), calls=%async_computation | async-start | bytes 393216 | tf_op jit(solution)/shard_map/all_to_all | solution.py:313
  20.4 9.3 %copy-start.1 = (f32[128,384]{1,0:T(8,128)S(1)}, f32[128,384]{1,0:T(8,128)}, u32[]{:S(2)}) copy-start(f32[128,384]{1,0:T(8,128)} %constant.10.clone.local) | copy-start | bytes 589828
  21.0 8.5 %collective-permute-start = (f32[45,8,128]{2,1,0:T(8,128)S(1)}, f32[45,8,128]{2,1,0:T(8,128)S(1)}, u32[]{:S(2)}, u32[]{:S(2)}) collective-permute-start(f32[45,8,128]{2,1,0:T(8,128)S(1)} %get-tuple-element.11), channel_id=1, source_target_pairs={{2,0},{4,2},{6,4},{8,6},{10,8},{12,10},{14,12},{3,1},{5,3},{7,5},{... | collective-permute-start | bytes 552968 | tf_op jit(solution)/shard_map/ppermute | solution.py:307
  22.9 6.9 %collective-permute-start.1 = (f32[45,8,128]{2,1,0:T(8,128)S(1)}, f32[45,8,128]{2,1,0:T(8,128)S(1)}, u32[]{:S(2)}, u32[]{:S(2)}) collective-permute-start(f32[45,8,128]{2,1,0:T(8,128)S(1)} %get-tuple-element.12), channel_id=1, source_target_pairs={{0,2},{2,4},{4,6},{6,8},{8,10},{10,12},{12,14},{1,3},{3,5},{5,7},{... | collective-permute-start | bytes 552968 | tf_op jit(solution)/shard_map/ppermute | solution.py:308
  25.3 6.8 %copy-start.3 = (f32[128,128]{1,0:T(8,128)S(1)}, f32[128,128]{1,0:T(8,128)}, u32[]{:S(2)}) copy-start(f32[128,128]{1,0:T(8,128)} %constant.13.clone.weigh) | copy-start | bytes 196612
  25.3 6.8 %copy-start.6 = (f32[16,128]{1,0:T(8,128)S(1)}, f32[16,128]{1,0:T(8,128)}, u32[]{:S(2)}) copy-start(f32[16,128]{1,0:T(8,128)} %constant.14.clone.powers) | copy-start | bytes 24580
  25.4 9.1 %collective-permute-start.4 = (f32[8,768]{1,0:T(8,128)S(1)}, f32[8,768]{1,0:T(8,128)S(1)}, u32[]{:S(2)}, u32[]{:S(2)}) collective-permute-start(f32[8,768]{1,0:T(8,128)S(1)} %get-tuple-element.16), channel_id=1, source_target_pairs={{16,0},{32,16},{48,32},{64,48},{80,64},{96,80},{112,96},{128,112},... | collective-permute-start | bytes 73736 | tf_op jit(solution)/shard_map/ppermute | solution.py:312
  29.5 6.1 %collective-permute-start.3 = (f32[8,768]{1,0:T(8,128)S(1)}, f32[8,768]{1,0:T(8,128)S(1)}, u32[]{:S(2)}, u32[]{:S(2)}) collective-permute-start(f32[8,768]{1,0:T(8,128)S(1)} %get-tuple-element.16), channel_id=1, source_target_pairs={{0,16},{16,32},{32,48},{48,64},{64,80},{80,96},{96,112},{112,128},... | collective-permute-start | bytes 73736 | tf_op jit(solution)/shard_map/ppermute | solution.py:311
  32.1 0.7 %copy-start.7 = (s32[9]{0:T(128)S(1)}, s32[9]{0:T(128)}, u32[]{:S(2)}) copy-start(s32[9]{0:T(128)} %shifts.1) | copy-start | bytes 112
  35.6 17.4 %copy-start.5 = (f32[24,256]{1,0:T(8,128)S(1)}, f32[24,256]{1,0:T(8,128)}, u32[]{:S(2)}) copy-start(f32[24,256]{1,0:T(8,128)} %constant.12.clone.side) | copy-start | bytes 73732

commit v3 on v2

--- a/solution.py
+++ b/solution.py
@@ -23,7 +23,7 @@
 PIECE = 3
 SLOTS = RING * PIECE
 LANES = SLOTS * ROWS
-SENT = 40
+SENT = 36
 GRANT = 16 * 2**20
 
 
@@ -93,32 +93,60 @@
     )
 
 
+def split(a):
+    high = a.astype(jnp.bfloat16)
+    return high, (a - high.astype(jnp.float32)).astype(jnp.bfloat16)
+
+
+def dot3(a, b, contract):
+    (ah, al), (bh, bl) = split(a), split(b)
+
+    def one(x, y):
+        return lax.dot_general(x, y, (contract, ((), ())), preferred_element_type=jnp.float32)
+
+    return one(ah, bh) + (one(ah, bl) + one(al, bh))
+
+
 def row_index(shape):
     return lax.broadcasted_iota(jnp.int32, shape, len(shape) - 2)
 
 
-def edge_kernel(density, moments, facing, sems):
+def edge_kernel(density, moments, facing, held, sems):
     plane = 1 - lax.axis_index("axial")
-    copies = []
+    reads, writes = [], []
     for v in range(VARS):
         source = density.at[:, plane] if v == 0 else moments.at[:, v - 1, plane]
-        copies.append(
-            pltpu.make_async_copy(source, facing.at[pl.ds(v * INST, INST)], sems.at[v])
-        )
-    for copy in copies:
-        copy.start()
-    facing[PAIRS:SLOTS] = jnp.zeros((SLOTS - PAIRS, ROWS, WIDTH), jnp.float32)
-    for copy in copies:
-        copy.wait()
-
-
-def pack_kernel(density, moments, pick, first, last, cols, flux):
+        at = pl.ds(v * INST, INST)
+        reads.append(pltpu.make_async_copy(source, held.at[at], sems.at[v]))
+        writes.append(pltpu.make_async_copy(held.at[at], facing.at[at], sems.at[VARS + v]))
+    at = pl.ds(PAIRS, SLOTS - PAIRS)
+    for read in reads:
+        read.start()
+    held[PAIRS:SLOTS] = jnp.zeros((SLOTS - PAIRS, ROWS, WIDTH), jnp.float32)
+    writes.append(pltpu.make_async_copy(held.at[at], facing.at[at], sems.at[2 * VARS]))
+    for read, write in zip(reads, writes):
+        read.wait()
+        write.start()
+    writes[-1].start()
+    for write in writes:
+        write.wait()
+
+
+def pack_kernel(shifts, density, moments, pick, inside, outside, cols, turns, flux):
+    axial, place = lax.axis_index("axial"), lax.axis_index("pitch")
+    extent = WIDTH * RING
+    for j in range(PIECE):
+        shift = shifts[lax.rem(place * PIECE + j, INST)]
+        turns[j] = jnp.where(axial == 1, shift, (extent - shift) & (extent - 1))
+    even = lax.rem(lax.axis_index("radial"), 2) == 0
     low = row_index((INST, ROWS, WIDTH)) < 4
     for v in range(VARS):
         one, two = field(density, moments, v, 0), field(density, moments, v, 1)
         at = slice(v * INST, (v + 1) * INST)
-        first[at] = jnp.where(low, one, pltpu.roll(two, 4, 1))
-        last[at] = jnp.where(low, pltpu.roll(one, 4, 1), two)
+        first = jnp.where(low, one, pltpu.roll(two, 4, 1))
+        last = jnp.where(low, pltpu.roll(one, 4, 1), two)
+        inside[at] = jnp.where(even, last, first)
+        outside[at] = jnp.where(even, first, last)
     for a in range(PLANES):
         along = fluxes(*[field(density, moments, v, a) for v in range(VARS)], 2)
         put(flux, a, along)
@@ -144,9 +172,10 @@
     return (mp, ma * speed, mr * speed, mp * speed + pressure, total * speed)
 
 
-def main_kernel(density, moments, above, below, local, pick, res, upd, sums, flux, rest):
+def main_kernel(density, moments, inside, outside, local, pick, res, upd, sums, flux, rest):
     axial = lax.axis_index("axial")
     radial = lax.axis_index("radial")
+    even = lax.rem(radial, 2) == 0
     shape = (INST, ROWS, WIDTH)
     row = row_index(shape)
     low = row < 4
@@ -157,7 +186,8 @@
         rims = []
         for v in range(VARS):
             at = slice(v * INST, (v + 1) * INST)
-            up, down = above[at], below[at]
+            near, far = inside[at], outside[at]
+            up, down = jnp.where(even, near, far), jnp.where(even, far, near)
             if a == 0:
                 rims.append(jnp.where(low, up, pltpu.roll(down, 4, 1)))
             else:
@@ -188,17 +218,13 @@
     )
 
 
-def align_kernel(shifts, whole, sums, weigh, powers, out, rolled, kept):
+def align_kernel(turns, whole, sums, weigh, powers, out, rolled, kept):
     axial = lax.axis_index("axial")
     place = lax.axis_index("pitch")
-    extent = WIDTH * RING
     tall = PIECE * ROWS
     lane = lax.broadcasted_iota(jnp.int32, (ROWS, WIDTH), 1)
     for j in range(PIECE):
-        inst = lax.rem(place * PIECE + j, INST)
-        shift = shifts[inst]
-        offset = jnp.where(axial == 1, shift, (extent - shift) & (extent - 1))
-        blocks, within = offset >> 7, offset & (WIDTH - 1)
+        blocks, within = turns[j] >> 7, turns[j] & (WIDTH - 1)
         turned = pltpu.roll(whole[:, j], within, 2)
         rolled[0:RING] = turned
         rolled[RING : 2 * RING] = turned
@@ -210,7 +236,7 @@
             out[at : at + ROWS] = window
             at = d * tall + j * ROWS
             kept[at : at + ROWS] = window
-    totals = dot(kept[...], weigh[...], ((1,), (0,)))
+    totals = dot3(kept[...], weigh[...], ((1,), (0,)))
     carried = totals[0:tall] * powers[0:1]
     for d in range(1, RING):
         carried = carried + totals[d * tall : (d + 1) * tall] * powers[d : d + 1]
@@ -227,7 +253,7 @@
     spots = lax.broadcasted_iota(jnp.int32, (tall, 2 * LANES), 1)
     select = (spots == target + row_index((tall, 2 * LANES))).astype(jnp.float32)
     right = jnp.concatenate([select, pltpu.roll(sums[...], 2, 0)], axis=0)
-    carries = dot(left, right, ((0,), (0,)))
+    carries = dot3(left[:, 0 : 2 * RING], right, ((0,), (0,)))
     for t in range(6):
         at = slice(t * WIDTH, (t + 1) * WIDTH)
         out[pl.ds(tall + t, RING, SENT)] = carries[0:RING, at]
@@ -237,9 +263,11 @@
 def final_kernel(res, upd, got, left, right, local, side, residual, update, first, second, sems):
     axial = lax.axis_index("axial")
     tall = PIECE * ROWS
-    windows = got[:, 0:tall].reshape(LANES, WIDTH)
-    smoothed = dot(windows, local[:, 2 * WIDTH :], ((1,), (0,)))
-    carries = jnp.sum(got[:, tall:SENT], axis=0)
+    windows = jnp.concatenate([got[h * SENT : h * SENT + tall] for h in range(RING)], axis=0)
+    smoothed = dot3(windows, local[:, 2 * WIDTH :], ((1,), (0,)))
+    carries = got[tall:SENT]
+    for h in range(1, RING):
+        carries = carries + got[h * SENT + tall : (h + 1) * SENT]
     line = row_index((8, WIDTH))
     copies = []
     for t in range(6):
@@ -249,7 +277,7 @@
             line == 0, carries[t : t + 1], jnp.where(line == 1, carries[6 + t : 7 + t], 0.0)
         )
         sides = jnp.concatenate([left[:, at], right[:, at], pair], axis=0)
-        added = dot(sides, side[...], ((0,), (0,)))
+        added = dot3(sides, side[...], ((0,), (0,)))
         mine = axial == 1 - a
         here = slice(part * WIDTH, (part + 1) * WIDTH)
         r = res[at] + added[:, 0:WIDTH] + jnp.where(mine, windows[here], 0.0)
@@ -290,22 +318,35 @@
         edge_kernel,
         out_shape=jax.ShapeDtypeStruct((SLOTS, ROWS, WIDTH), jnp.float32),
         in_specs=[pl.BlockSpec(memory_space=pl.ANY)] * 2,
-        out_specs=pl.BlockSpec(memory_space=pltpu.VMEM),
-        scratch_shapes=[pltpu.SemaphoreType.DMA((VARS,))],
+        out_specs=pl.BlockSpec(memory_space=pl.ANY),
+        scratch_shapes=[
+            pltpu.VMEM((SLOTS, ROWS, WIDTH), jnp.float32),
+            pltpu.SemaphoreType.DMA((2 * VARS + 1,)),
+        ],
     )(density, moments)
     across = lax.ppermute(facing, "axial", [(0, 1), (1, 0)])
-    first, last, cols = call(
+    vmem = pl.BlockSpec(memory_space=pltpu.VMEM)
+    smem = pl.BlockSpec(memory_space=pltpu.SMEM)
+    halo = jax.ShapeDtypeStruct((PAIRS, ROWS, WIDTH), jnp.float32)
+    inside, outside, cols, turns = pl.pallas_call(
         pack_kernel,
-        [(PAIRS, ROWS, WIDTH), (PAIRS, ROWS, WIDTH), (8, height)],
-        scratch=[(height, WIDTH)],
-        inputs=3,
-        work=(10**6, 10**6),
-    )(density, moments, pick)
+        out_shape=[
+            halo,
+            halo,
+            jax.ShapeDtypeStruct((8, height), jnp.float32),
+            jax.ShapeDtypeStruct((PIECE,), jnp.int32),
+        ],
+        in_specs=[smem, vmem, vmem, vmem],
+        out_specs=[vmem, vmem, vmem, smem],
+        scratch_shapes=[pltpu.VMEM((height, WIDTH), jnp.float32)],
+        cost_estimate=pl.CostEstimate(flops=10**6, bytes_accessed=10**6, transcendentals=0),
+        compiler_params=pltpu.CompilerParams(vmem_limit_bytes=GRANT),
+    )(shifts, density, moments, pick)
     count_r = lax.axis_size("radial")
-    up = [(i, i + 1) for i in range(count_r - 1)]
-    down = [(j, i) for i, j in up]
-    above = lax.ppermute(first, "radial", down)
-    below = lax.ppermute(last, "radial", up)
+    pairs = [(i, i ^ 1) for i in range(count_r)]
+    between = [(i, i - 1 if i % 2 == 0 else i + 1) for i in range(1, count_r - 1)]
+    inside = lax.ppermute(inside, "radial", pairs)
+    outside = lax.ppermute(outside, "radial", between)
     ring = [(i, (i + 1) % RING) for i in range(RING)]
     back = [(j, i) for i, j in ring]
     left = lax.ppermute(cols, "pitch", ring)
@@ -317,7 +358,7 @@
         scratch=[(height, WIDTH), (height, WIDTH)],
         inputs=6,
         work=(10**8, 2 * 10**6),
-    )(density, moments, above, below, local, pick)
+    )(density, moments, inside, outside, local, pick)
     (send,) = call(
         align_kernel,
         [(RING * SENT, WIDTH)],
@@ -325,9 +366,10 @@
         scalars=1,
         inputs=4,
         work=(10**7, 10**6),
-    )(shifts, whole, sums, weigh, powers)
+    )(turns, whole, sums, weigh, powers)
     send, left, right = lax.optimization_barrier((send, left, right))
-    got = lax.all_to_all(send.reshape(RING, SENT, WIDTH), "pitch", 0, 0)
+    got = lax.all_to_all(send.reshape(RING, SENT // 4, 4, WIDTH), "pitch", 0, 0)
+    got = got.reshape(RING * SENT, WIDTH)
     shape = (INST, VARS, PLANES, ROWS, WIDTH)
     held = pltpu.VMEM((PLANES, INST, VARS, ROWS, WIDTH), jnp.float32)
     return pl.pallas_call(

time: 55.6 us -> 53.2 us (0.957)
  starting transfers between devices: 21.2 us -> 19.4 us
  waiting for transfers between devices: 6.91 us -> 7.98 us
  local copies, waits for them, and re-layouts: 0.67 us -> 0.04 us
    ppermute x2, starting transfers between devices: 4.34 us -> 2.54 us  [the longest x1 2.45 us: local_step(): outside = lax.ppermute(outside, 'radial', between)]
    ppermute x1, waiting for transfers between devices: 1.17 us -> 2.27 us  [local_step(): left = lax.ppermute(cols, 'pitch', ring)]
    pallas_call x1, Pallas kernels: 0.53 us -> 1.19 us  [local_step(): pl.pallas_call(pack_kernel, out_shape=[halo, halo, jax.ShapeDtypeStruct((...]
    unnamed x16, local copies, waits for them, and re-layouts: 0.67 us -> 0.04 us
  transfers between devices with their start and end apart: 6 -> 6, of which waited for: 3 -> 3; matrix products, arithmetic and copies ran while one was open for 0% -> 0% of each run, Pallas kernels for 8% -> 9%
where the time goes in v3:
time: 53.2 us; the launch traced here: 52.7 us
  starting transfers between devices  19.4 us (36%)
  blocking collectives  16.9 us (32%)
  waiting for transfers between devices  7.98 us (15%)
  Pallas kernels  7.65 us (14%)
  between operations  0.76 us (1%)
    all_to_all x1, blocking collectives, local_step(): got = lax.all_to_all(send.reshape(RING, SENT // 4, 4, WIDTH), 'pitch', 0, 0)  16.9 us
    all_to_all x1, starting transfers between devices, local_step(): lax.all_to_all(across.reshape(RING, PIECE, ROWS, WIDTH), 'pitch', 0, 0)  9.63 us
    ppermute x1, waiting for transfers between devices, local_step(): across = lax.ppermute(facing, 'axial', [(0, 1), (1, 0)])  5.44 us
    ppermute x1, starting transfers between devices, local_step(): right = lax.ppermute(cols, 'pitch', back)  4.11 us
    ppermute x1, starting transfers between devices, local_step(): across = lax.ppermute(facing, 'axial', [(0, 1), (1, 0)])  3.11 us
    ppermute x1, starting transfers between devices, local_step(): outside = lax.ppermute(outside, 'radial', between)  2.45 us
    pallas_call x1, Pallas kernels, local_step(): call(main_kernel, [(height, WIDTH), (height, WIDTH), (8, height)], scratc...  2.34 us
    ppermute x1, waiting for transfers between devices, local_step(): left = lax.ppermute(cols, 'pitch', ring)  2.27 us
  transfers between devices with their start and end apart: 6, of which 3 were waited for; matrix products, arithmetic and copies ran while one was open for 0% of the time, Pallas kernels for 9%

profile of v3, /device:TPU:8, one launch (start us, length us, event | category | flops | bytes accessed | tf_op | source)
XLA Modules:
  0.0 52.7 jit_solution(10742623913177065249)
XLA Ops:
  0.6 1.6 %shard_map.97 = f32[48,8,128]{2,1,0:T(8,128)} custom-call(f32[9,2,8,128]{3,2,1,0:T(8,128)} %density.5, f32[9,4,2,8,128]{4,3,2,1,0:T(8,128)} %moments.5), custom_call_target="tpu_custom_call" | custom-call | tf_op jit(solution)/shard_map/pallas_call | solution.py:317
  2.2 0.0 copy-start
  2.2 3.1 %collective-permute-start.2 = (f32[48,8,128]{2,1,0:T(8,128)}, f32[48,8,128]{2,1,0:T(8,128)}, u32[]{:S(2)}, u32[]{:S(2)}) collective-permute-start(f32[48,8,128]{2,1,0:T(8,128)} %shard_map.97), channel_id=1, source_target_pairs={{0,1},{1,0},{2,3},{3,2},{4,5},{5,4},{6,7},{7,6},{8,9},{9,8},{10,11... | collective-permute-start | bytes 589832 | tf_op jit(solution)/shard_map/ppermute | solution.py:327
  5.3 5.4 %collective-permute-done.2 = f32[48,8,128]{2,1,0:T(8,128)} collective-permute-done((f32[48,8,128]{2,1,0:T(8,128)}, f32[48,8,128]{2,1,0:T(8,128)}, u32[]{:S(2)}, u32[]{:S(2)}) %collective-permute-start.2) | collective-permute-done | bytes 196640 | tf_op jit(solution)/shard_map/ppermute | solution.py:327
  10.8 0.0 copy-start.2
  10.8 0.0 copy-start.4
  10.8 0.0 copy-start.7
  10.8 9.6 %all-to-all-start = ((f32[16,3,8,128]{3,2,1,0:T(8,128)}), f32[16,3,8,128]{3,2,1,0:T(8,128)S(1)}, u32[]{:S(2)}, u32[]{:S(2)}) async-start(f32[16,3,8,128]{3,2,1,0:T(8,128)} %bitcast), calls=%async_computation | async-start | bytes 393216 | tf_op jit(solution)/shard_map/all_to_all | solution.py:354
  20.4 0.0 copy-done
  20.4 0.0 copy-done.2
  20.4 0.0 copy-done.4
  20.4 0.0 copy-done.7
  20.4 0.0 copy-start.1
  20.5 1.2 %shard_map.95 = (f32[45,8,128]{2,1,0:T(8,128)S(1)}, f32[45,8,128]{2,1,0:T(8,128)S(1)}, f32[8,768]{1,0:T(8,128)S(1)}, s32[3]{0:T(128)S(1)}) custom-call(s32[9]{0:T(128)S(1)} %copy-done.7, f32[9,2,8,128]{3,2,1,0:T(8,128)S(1)} %copy-done.2, f32[9,4,2,8,128]{4,3,2,1,0:T(8,128)S(1)} %copy-done, f32[16,128]{1,0:T(8,128)S(1)} %copy-done.4), custom_call_target="tpu_custom_call" | custom-call | flops 1000000 | bytes 1000000 | tf_op jit(solution)/shard_map/pallas_call | solution.py:331
  21.7 0.1 collective-permute-start
  21.8 2.4 %collective-permute-start.1 = (f32[45,8,128]{2,1,0:T(8,128)S(1)}, f32[45,8,128]{2,1,0:T(8,128)S(1)}, u32[]{:S(2)}, u32[]{:S(2)}) collective-permute-start(f32[45,8,128]{2,1,0:T(8,128)S(1)} %get-tuple-element.13), channel_id=1, source_target_pairs={{2,4},{4,2},{6,8},{8,6},{10,12},{12,10},{3,5},{5,3},{7,9},{9,7},{1... | collective-permute-start | bytes 552968 | tf_op jit(solution)/shard_map/ppermute | solution.py:349
  24.2 0.0 copy-start.3
  24.2 4.1 %collective-permute-start.4 = (f32[8,768]{1,0:T(8,128)S(1)}, f32[8,768]{1,0:T(8,128)S(1)}, u32[]{:S(2)}, u32[]{:S(2)}) collective-permute-start(f32[8,768]{1,0:T(8,128)S(1)} %get-tuple-element.18), channel_id=1, source_target_pairs={{16,0},{32,16},{48,32},{64,48},{80,64},{96,80},{112,96},{128,112},... | collective-permute-start | bytes 73736 | tf_op jit(solution)/shard_map/ppermute | solution.py:353
  28.3 0.0 collective-permute-start.3
  28.3 0.0 collective-permute-done.inside
  28.3 0.3 collective-permute-done.1.outside
  28.6 0.0 copy-done.1
  28.6 0.0 copy-start.6
  28.6 2.3 %shard_map.96 = (f32[768,128]{1,0:T(8,128)S(1)}, f32[768,128]{1,0:T(8,128)S(1)}, f32[8,768]{1,0:T(8,128)S(1)}) custom-call(f32[9,2,8,128]{3,2,1,0:T(8,128)S(1)} %copy-done.2, f32[9,4,2,8,128]{4,3,2,1,0:T(8,128)S(1)} %copy-done, f32[45,8,128]{2,1,0:T(8,128)S(1)} %collective-permute-done.inside, f32[45,8,128]{2,1,0:T(8,128)S(1)} %collective-permute-done.1.outside, ...), custom_call_target="tpu_custom_call" | custom-call | flops 100000000 | bytes 2000000 | tf_op jit(solution)/shard_map/pallas_call | solution.py:355
  31.0 0.0 all-to-all-done.whole
  31.0 0.0 copy-done.3
  31.0 0.0 copy-done.6
  31.0 1.2 %shard_map.98 = f32[576,128]{1,0:T(8,128)S(1)} custom-call(s32[3]{0:T(128)S(1)} %get-tuple-element.16.turns, f32[16,3,8,128]{3,2,1,0:T(8,128)S(1)} %all-to-all-done.whole, f32[8,768]{1,0:T(8,128)S(1)} %get-tuple-element.17.sums, f32[128,128]{1,0:T(8,128)S(1)} %copy-done.3, f32[16,128]{1,0:T(8,128)S(1)} %copy-done.6), custom_call_target="tpu_custom_call" | custom-call | flops 10000000 | bytes 1000000 | tf_op jit(solution)/shard_map/pallas_call | solution.py:362
  32.2 0.0 collective-permute-done.4.right
  32.2 2.3 %collective-permute-done.3.left = f32[8,768]{1,0:T(8,128)S(1)} collective-permute-done((f32[8,768]{1,0:T(8,128)S(1)}, f32[8,768]{1,0:T(8,128)S(1)}, u32[]{:S(2)}, u32[]{:S(2)}) %collective-permute-start.3) | collective-permute-done | bytes 24608 | tf_op jit(solution)/shard_map/ppermute | solution.py:352
  34.4 0.0 copy-start.5
  34.4 16.9 %all_to_all.10 = f32[16,9,4,128]{3,2,1,0:T(4,128)S(1)} all-to-all(f32[16,9,4,128]{3,2,1,0:T(4,128)S(1)} %bitcast.3), channel_id=1, replica_groups=mesh['pitch'=16,'radial'=8,'axial'=2] {'pitch'}, dimensions={0} | all-to-all | bytes 589824 | tf_op jit(solution)/shard_map/all_to_all | solution.py:371
  51.4 0.0 copy-done.5
  51.4 1.4 %shard_map.99 = (f32[9,5,2,8,128]{4,3,2,1,0:T(8,128)}, f32[9,5,2,8,128]{4,3,2,1,0:T(8,128)}) custom-call(f32[768,128]{1,0:T(8,128)S(1)} %get-tuple-element.14.res, f32[768,128]{1,0:T(8,128)S(1)} %get-tuple-element.15.upd, f32[576,128]{1,0:T(8,128)S(1)} %bitcast.4, f32[8,768]{1,0:T(8,128)S(1)} %collective-permute-done.3.left, ...), custom_call_target="tpu_custom_call" | custom-call | flops 10000000 | bytes 2000000 | tf_op jit(solution)/shard_map/pallas_call | solution.py:375
Async XLA Ops:
  2.2 18.2 %copy-start = (f32[9,4,2,8,128]{4,3,2,1,0:T(8,128)S(1)}, f32[9,4,2,8,128]{4,3,2,1,0:T(8,128)}, u32[]{:S(2)}) copy-start(f32[9,4,2,8,128]{4,3,2,1,0:T(8,128)} %moments.5) | copy-start | bytes 884740
  2.2 8.5 %collective-permute-start.2 = (f32[48,8,128]{2,1,0:T(8,128)}, f32[48,8,128]{2,1,0:T(8,128)}, u32[]{:S(2)}, u32[]{:S(2)}) collective-permute-start(f32[48,8,128]{2,1,0:T(8,128)} %shard_map.97), channel_id=1, source_target_pairs={{0,1},{1,0},{2,3},{3,2},{4,5},{5,4},{6,7},{7,6},{8,9},{9,8},{10,11... | collective-permute-start | bytes 589832 | tf_op jit(solution)/shard_map/ppermute | solution.py:327
  10.8 9.7 %copy-start.2 = (f32[9,2,8,128]{3,2,1,0:T(8,128)S(1)}, f32[9,2,8,128]{3,2,1,0:T(8,128)}, u32[]{:S(2)}) copy-start(f32[9,2,8,128]{3,2,1,0:T(8,128)} %density.5) | copy-start | bytes 221188
  10.8 9.7 %copy-start.4 = (f32[16,128]{1,0:T(8,128)S(1)}, f32[16,128]{1,0:T(8,128)}, u32[]{:S(2)}) copy-start(f32[16,128]{1,0:T(8,128)} %constant.11.clone.pick) | copy-start | bytes 24580
  10.8 9.7 %copy-start.7 = (s32[9]{0:T(128)S(1)}, s32[9]{0:T(128)}, u32[]{:S(2)}) copy-start(s32[9]{0:T(128)} %shifts.1) | copy-start | bytes 112
  10.8 20.2 %all-to-all-start = ((f32[16,3,8,128]{3,2,1,0:T(8,128)}), f32[16,3,8,128]{3,2,1,0:T(8,128)S(1)}, u32[]{:S(2)}, u32[]{:S(2)}) async-start(f32[16,3,8,128]{3,2,1,0:T(8,128)} %bitcast), calls=%async_computation | async-start | bytes 393216 | tf_op jit(solution)/shard_map/all_to_all | solution.py:354
  20.4 8.2 %copy-start.1 = (f32[128,384]{1,0:T(8,128)S(1)}, f32[128,384]{1,0:T(8,128)}, u32[]{:S(2)}) copy-start(f32[128,384]{1,0:T(8,128)} %constant.10.clone.local) | copy-start | bytes 589828
  21.7 6.7 %collective-permute-start = (f32[45,8,128]{2,1,0:T(8,128)S(1)}, f32[45,8,128]{2,1,0:T(8,128)S(1)}, u32[]{:S(2)}, u32[]{:S(2)}) collective-permute-start(f32[45,8,128]{2,1,0:T(8,128)S(1)} %get-tuple-element.12), channel_id=1, source_target_pairs={{0,2},{2,0},{4,6},{6,4},{8,10},{10,8},{12,14},{14,12},{1,3},{3,1},... | collective-permute-start | bytes 552968 | tf_op jit(solution)/shard_map/ppermute | solution.py:348
  21.8 6.9 %collective-permute-start.1 = (f32[45,8,128]{2,1,0:T(8,128)S(1)}, f32[45,8,128]{2,1,0:T(8,128)S(1)}, u32[]{:S(2)}, u32[]{:S(2)}) collective-permute-start(f32[45,8,128]{2,1,0:T(8,128)S(1)} %get-tuple-element.13), channel_id=1, source_target_pairs={{2,4},{4,2},{6,8},{8,6},{10,12},{12,10},{3,5},{5,3},{7,9},{9,7},{1... | collective-permute-start | bytes 552968 | tf_op jit(solution)/shard_map/ppermute | solution.py:349
  24.2 6.7 %copy-start.3 = (f32[128,128]{1,0:T(8,128)S(1)}, f32[128,128]{1,0:T(8,128)}, u32[]{:S(2)}) copy-start(f32[128,128]{1,0:T(8,128)} %constant.13.clone.weigh) | copy-start | bytes 196612
  24.2 7.9 %collective-permute-start.4 = (f32[8,768]{1,0:T(8,128)S(1)}, f32[8,768]{1,0:T(8,128)S(1)}, u32[]{:S(2)}, u32[]{:S(2)}) collective-permute-start(f32[8,768]{1,0:T(8,128)S(1)} %get-tuple-element.18), channel_id=1, source_target_pairs={{16,0},{32,16},{48,32},{64,48},{80,64},{96,80},{112,96},{128,112},... | collective-permute-start | bytes 73736 | tf_op jit(solution)/shard_map/ppermute | solution.py:353
  28.3 6.1 %collective-permute-start.3 = (f32[8,768]{1,0:T(8,128)S(1)}, f32[8,768]{1,0:T(8,128)S(1)}, u32[]{:S(2)}, u32[]{:S(2)}) collective-permute-start(f32[8,768]{1,0:T(8,128)S(1)} %get-tuple-element.18), channel_id=1, source_target_pairs={{0,16},{16,32},{32,48},{48,64},{64,80},{80,96},{96,112},{112,128},... | collective-permute-start | bytes 73736 | tf_op jit(solution)/shard_map/ppermute | solution.py:352
  28.6 2.3 %copy-start.6 = (f32[16,128]{1,0:T(8,128)S(1)}, f32[16,128]{1,0:T(8,128)}, u32[]{:S(2)}) copy-start(f32[16,128]{1,0:T(8,128)} %constant.14.clone.powers) | copy-start | bytes 24580
  34.4 16.9 %copy-start.5 = (f32[24,256]{1,0:T(8,128)S(1)}, f32[24,256]{1,0:T(8,128)}, u32[]{:S(2)}) copy-start(f32[24,256]{1,0:T(8,128)} %constant.12.clone.side) | copy-start | bytes 73732

commit v4 on v3

--- a/solution.py
+++ b/solution.py
@@ -111,25 +111,19 @@
     return lax.broadcasted_iota(jnp.int32, shape, len(shape) - 2)
 
 
-def edge_kernel(density, moments, facing, held, sems):
+def edge_kernel(density, moments, facing, sems):
     plane = 1 - lax.axis_index("axial")
-    reads, writes = [], []
+    copies = []
     for v in range(VARS):
         source = density.at[:, plane] if v == 0 else moments.at[:, v - 1, plane]
-        at = pl.ds(v * INST, INST)
-        reads.append(pltpu.make_async_copy(source, held.at[at], sems.at[v]))
-        writes.append(pltpu.make_async_copy(held.at[at], facing.at[at], sems.at[VARS + v]))
-    at = pl.ds(PAIRS, SLOTS - PAIRS)
-    for read in reads:
-        read.start()
-    held[PAIRS:SLOTS] = jnp.zeros((SLOTS - PAIRS, ROWS, WIDTH), jnp.float32)
-    writes.append(pltpu.make_async_copy(held.at[at], facing.at[at], sems.at[2 * VARS]))
-    for read, write in zip(reads, writes):
-        read.wait()
-        write.start()
-    writes[-1].start()
-    for write in writes:
-        write.wait()
+        copies.append(
+            pltpu.make_async_copy(source, facing.at[pl.ds(v * INST, INST)], sems.at[v])
+        )
+    for copy in copies:
+        copy.start()
+    facing[PAIRS:SLOTS] = jnp.zeros((SLOTS - PAIRS, ROWS, WIDTH), jnp.float32)
+    for copy in copies:
+        copy.wait()
 
 
 def pack_kernel(shifts, density, moments, pick, inside, outside, cols, turns, flux):
@@ -317,13 +311,11 @@
     facing = pl.pallas_call(
         edge_kernel,
         out_shape=jax.ShapeDtypeStruct((SLOTS, ROWS, WIDTH), jnp.float32),
-        in_specs=[pl.BlockSpec(memory_space=pl.ANY)] * 2,
-        out_specs=pl.BlockSpec(memory_space=pl.ANY),
-        scratch_shapes=[
-            pltpu.VMEM((SLOTS, ROWS, WIDTH), jnp.float32),
-            pltpu.SemaphoreType.DMA((2 * VARS + 1,)),
-        ],
-    )(density, moments)
+        in_specs=[pl.BlockSpec(memory_space=pltpu.HBM)] * 2,
+        out_specs=pl.BlockSpec(memory_space=pltpu.VMEM),
+        scratch_shapes=[pltpu.SemaphoreType.DMA((VARS,))],
+        compiler_params=pltpu.CompilerParams(vmem_limit_bytes=16 * 2**20),
+    )(*[pltpu.with_memory_space_constraint(x, pltpu.HBM) for x in (density, moments)])
     across = lax.ppermute(facing, "axial", [(0, 1), (1, 0)])
     vmem = pl.BlockSpec(memory_space=pltpu.VMEM)
     smem = pl.BlockSpec(memory_space=pltpu.SMEM)

time: 53.2 us -> 52.4 us (0.985)
  Pallas kernels: 7.65 us -> 6.98 us
    pallas_call x1, Pallas kernels: 1.56 us -> 0.89 us  [local_step(): pl.pallas_call(edge_kernel, out_shape=jax.ShapeDtypeStruct((SLOTS, ROWS,...]
where the time goes in v4:
time: 52.4 us; the launch traced here: 51.8 us
  starting transfers between devices  19.4 us (37%)
  blocking collectives  16.9 us (32%)
  waiting for transfers between devices  7.78 us (15%)
  Pallas kernels  6.98 us (13%)
  between operations  0.76 us (1%)
    all_to_all x1, blocking collectives, local_step(): got = lax.all_to_all(send.reshape(RING, SENT // 4, 4, WIDTH), 'pitch', 0, 0)  16.9 us
    all_to_all x1, starting transfers between devices, local_step(): lax.all_to_all(across.reshape(RING, PIECE, ROWS, WIDTH), 'pitch', 0, 0)  9.63 us
    ppermute x1, waiting for transfers between devices, local_step(): across = lax.ppermute(facing, 'axial', [(0, 1), (1, 0)])  5.23 us
    ppermute x1, starting transfers between devices, local_step(): right = lax.ppermute(cols, 'pitch', back)  4.11 us
    ppermute x1, starting transfers between devices, local_step(): across = lax.ppermute(facing, 'axial', [(0, 1), (1, 0)])  3.11 us
    ppermute x1, starting transfers between devices, local_step(): outside = lax.ppermute(outside, 'radial', between)  2.45 us
    pallas_call x1, Pallas kernels, local_step(): call(main_kernel, [(height, WIDTH), (height, WIDTH), (8, height)], scratc...  2.33 us
    ppermute x1, waiting for transfers between devices, local_step(): left = lax.ppermute(cols, 'pitch', ring)  2.27 us
  transfers between devices with their start and end apart: 6, of which 3 were waited for; matrix products, arithmetic and copies ran while one was open for 0% of the time, Pallas kernels for 9%

profile of v4, /device:TPU:8, one launch (start us, length us, event | category | flops | bytes accessed | tf_op | source)
XLA Modules:
  0.0 51.8 jit_solution(291321945084948295)
XLA Ops:
  0.6 0.9 %shard_map.97 = f32[48,8,128]{2,1,0:T(8,128)S(1)} custom-call(f32[9,2,8,128]{3,2,1,0:T(8,128)} %density.5, f32[9,4,2,8,128]{4,3,2,1,0:T(8,128)} %moments.5), custom_call_target="tpu_custom_call" | custom-call | tf_op jit(solution)/shard_map/pallas_call | solution.py:311
  1.5 0.0 copy-start
  1.5 3.1 %collective-permute-start.2 = (f32[48,8,128]{2,1,0:T(8,128)S(1)}, f32[48,8,128]{2,1,0:T(8,128)}, u32[]{:S(2)}, u32[]{:S(2)}) collective-permute-start(f32[48,8,128]{2,1,0:T(8,128)S(1)} %shard_map.97), channel_id=1, source_target_pairs={{0,1},{1,0},{2,3},{3,2},{4,5},{5,4},{6,7},{7,6},{8,9},{9,8},{10,11... | collective-permute-start | bytes 589832 | tf_op jit(solution)/shard_map/ppermute | solution.py:319
  4.7 5.2 %collective-permute-done.2 = f32[48,8,128]{2,1,0:T(8,128)} collective-permute-done((f32[48,8,128]{2,1,0:T(8,128)S(1)}, f32[48,8,128]{2,1,0:T(8,128)}, u32[]{:S(2)}, u32[]{:S(2)}) %collective-permute-start.2) | collective-permute-done | bytes 196640 | tf_op jit(solution)/shard_map/ppermute | solution.py:319
  9.9 0.0 copy-start.2
  9.9 0.0 copy-start.4
  9.9 0.0 copy-start.7
  9.9 9.6 %all-to-all-start = ((f32[16,3,8,128]{3,2,1,0:T(8,128)}), f32[16,3,8,128]{3,2,1,0:T(8,128)S(1)}, u32[]{:S(2)}, u32[]{:S(2)}) async-start(f32[16,3,8,128]{3,2,1,0:T(8,128)} %bitcast), calls=%async_computation | async-start | bytes 393216 | tf_op jit(solution)/shard_map/all_to_all | solution.py:346
  19.5 0.0 copy-done
  19.5 0.0 copy-done.2
  19.5 0.0 copy-done.4
  19.6 0.0 copy-done.7
  19.6 0.0 copy-start.1
  19.6 1.2 %shard_map.95 = (f32[45,8,128]{2,1,0:T(8,128)S(1)}, f32[45,8,128]{2,1,0:T(8,128)S(1)}, f32[8,768]{1,0:T(8,128)S(1)}, s32[3]{0:T(128)S(1)}) custom-call(s32[9]{0:T(128)S(1)} %copy-done.7, f32[9,2,8,128]{3,2,1,0:T(8,128)S(1)} %copy-done.2, f32[9,4,2,8,128]{4,3,2,1,0:T(8,128)S(1)} %copy-done, f32[16,128]{1,0:T(8,128)S(1)} %copy-done.4), custom_call_target="tpu_custom_call" | custom-call | flops 1000000 | bytes 1000000 | tf_op jit(solution)/shard_map/pallas_call | solution.py:323
  20.8 0.1 collective-permute-start
  20.9 2.4 %collective-permute-start.1 = (f32[45,8,128]{2,1,0:T(8,128)S(1)}, f32[45,8,128]{2,1,0:T(8,128)S(1)}, u32[]{:S(2)}, u32[]{:S(2)}) collective-permute-start(f32[45,8,128]{2,1,0:T(8,128)S(1)} %get-tuple-element.13), channel_id=1, source_target_pairs={{2,4},{4,2},{6,8},{8,6},{10,12},{12,10},{3,5},{5,3},{7,9},{9,7},{1... | collective-permute-start | bytes 552968 | tf_op jit(solution)/shard_map/ppermute | solution.py:341
  23.3 0.0 copy-start.3
  23.3 4.1 %collective-permute-start.4 = (f32[8,768]{1,0:T(8,128)S(1)}, f32[8,768]{1,0:T(8,128)S(1)}, u32[]{:S(2)}, u32[]{:S(2)}) collective-permute-start(f32[8,768]{1,0:T(8,128)S(1)} %get-tuple-element.18), channel_id=1, source_target_pairs={{16,0},{32,16},{48,32},{64,48},{80,64},{96,80},{112,96},{128,112},... | collective-permute-start | bytes 73736 | tf_op jit(solution)/shard_map/ppermute | solution.py:345
  27.5 0.0 collective-permute-start.3
  27.5 0.0 collective-permute-done.inside
  27.5 0.3 collective-permute-done.1.outside
  27.7 0.0 copy-done.1
  27.7 0.0 copy-start.6
  27.7 2.3 %shard_map.96 = (f32[768,128]{1,0:T(8,128)S(1)}, f32[768,128]{1,0:T(8,128)S(1)}, f32[8,768]{1,0:T(8,128)S(1)}) custom-call(f32[9,2,8,128]{3,2,1,0:T(8,128)S(1)} %copy-done.2, f32[9,4,2,8,128]{4,3,2,1,0:T(8,128)S(1)} %copy-done, f32[45,8,128]{2,1,0:T(8,128)S(1)} %collective-permute-done.inside, f32[45,8,128]{2,1,0:T(8,128)S(1)} %collective-permute-done.1.outside, ...), custom_call_target="tpu_custom_call" | custom-call | flops 100000000 | bytes 2000000 | tf_op jit(solution)/shard_map/pallas_call | solution.py:347
  30.1 0.0 all-to-all-done.whole
  30.1 0.0 copy-done.3
  30.1 0.0 copy-done.6
  30.1 1.2 %shard_map.98 = f32[576,128]{1,0:T(8,128)S(1)} custom-call(s32[3]{0:T(128)S(1)} %get-tuple-element.16.turns, f32[16,3,8,128]{3,2,1,0:T(8,128)S(1)} %all-to-all-done.whole, f32[8,768]{1,0:T(8,128)S(1)} %get-tuple-element.17.sums, f32[128,128]{1,0:T(8,128)S(1)} %copy-done.3, f32[16,128]{1,0:T(8,128)S(1)} %copy-done.6), custom_call_target="tpu_custom_call" | custom-call | flops 10000000 | bytes 1000000 | tf_op jit(solution)/shard_map/pallas_call | solution.py:354
  31.3 0.0 collective-permute-done.4.right
  31.3 2.3 %collective-permute-done.3.left = f32[8,768]{1,0:T(8,128)S(1)} collective-permute-done((f32[8,768]{1,0:T(8,128)S(1)}, f32[8,768]{1,0:T(8,128)S(1)}, u32[]{:S(2)}, u32[]{:S(2)}) %collective-permute-start.3) | collective-permute-done | bytes 24608 | tf_op jit(solution)/shard_map/ppermute | solution.py:344
  33.6 0.0 copy-start.5
  33.6 16.9 %all_to_all.10 = f32[16,9,4,128]{3,2,1,0:T(4,128)S(1)} all-to-all(f32[16,9,4,128]{3,2,1,0:T(4,128)S(1)} %bitcast.3), channel_id=1, replica_groups=mesh['pitch'=16,'radial'=8,'axial'=2] {'pitch'}, dimensions={0} | all-to-all | bytes 589824 | tf_op jit(solution)/shard_map/all_to_all | solution.py:363
  50.5 0.0 copy-done.5
  50.5 1.4 %shard_map.99 = (f32[9,5,2,8,128]{4,3,2,1,0:T(8,128)}, f32[9,5,2,8,128]{4,3,2,1,0:T(8,128)}) custom-call(f32[768,128]{1,0:T(8,128)S(1)} %get-tuple-element.14.res, f32[768,128]{1,0:T(8,128)S(1)} %get-tuple-element.15.upd, f32[576,128]{1,0:T(8,128)S(1)} %bitcast.4, f32[8,768]{1,0:T(8,128)S(1)} %collective-permute-done.3.left, ...), custom_call_target="tpu_custom_call" | custom-call | flops 10000000 | bytes 2000000 | tf_op jit(solution)/shard_map/pallas_call | solution.py:367
Async XLA Ops:
  1.5 18.0 %copy-start = (f32[9,4,2,8,128]{4,3,2,1,0:T(8,128)S(1)}, f32[9,4,2,8,128]{4,3,2,1,0:T(8,128)}, u32[]{:S(2)}) copy-start(f32[9,4,2,8,128]{4,3,2,1,0:T(8,128)} %moments.5) | copy-start | bytes 884740
  1.5 8.3 %collective-permute-start.2 = (f32[48,8,128]{2,1,0:T(8,128)S(1)}, f32[48,8,128]{2,1,0:T(8,128)}, u32[]{:S(2)}, u32[]{:S(2)}) collective-permute-start(f32[48,8,128]{2,1,0:T(8,128)S(1)} %shard_map.97), channel_id=1, source_target_pairs={{0,1},{1,0},{2,3},{3,2},{4,5},{5,4},{6,7},{7,6},{8,9},{9,8},{10,11... | collective-permute-start | bytes 589832 | tf_op jit(solution)/shard_map/ppermute | solution.py:319
  9.9 9.7 %copy-start.2 = (f32[9,2,8,128]{3,2,1,0:T(8,128)S(1)}, f32[9,2,8,128]{3,2,1,0:T(8,128)}, u32[]{:S(2)}) copy-start(f32[9,2,8,128]{3,2,1,0:T(8,128)} %density.5) | copy-start | bytes 221188
  9.9 9.7 %copy-start.4 = (f32[16,128]{1,0:T(8,128)S(1)}, f32[16,128]{1,0:T(8,128)}, u32[]{:S(2)}) copy-start(f32[16,128]{1,0:T(8,128)} %constant.11.clone.pick) | copy-start | bytes 24580
  9.9 9.7 %copy-start.7 = (s32[9]{0:T(128)S(1)}, s32[9]{0:T(128)}, u32[]{:S(2)}) copy-start(s32[9]{0:T(128)} %shifts.1) | copy-start | bytes 112
  9.9 20.2 %all-to-all-start = ((f32[16,3,8,128]{3,2,1,0:T(8,128)}), f32[16,3,8,128]{3,2,1,0:T(8,128)S(1)}, u32[]{:S(2)}, u32[]{:S(2)}) async-start(f32[16,3,8,128]{3,2,1,0:T(8,128)} %bitcast), calls=%async_computation | async-start | bytes 393216 | tf_op jit(solution)/shard_map/all_to_all | solution.py:346
  19.6 8.2 %copy-start.1 = (f32[128,384]{1,0:T(8,128)S(1)}, f32[128,384]{1,0:T(8,128)}, u32[]{:S(2)}) copy-start(f32[128,384]{1,0:T(8,128)} %constant.10.clone.local) | copy-start | bytes 589828
  20.8 6.7 %collective-permute-start = (f32[45,8,128]{2,1,0:T(8,128)S(1)}, f32[45,8,128]{2,1,0:T(8,128)S(1)}, u32[]{:S(2)}, u32[]{:S(2)}) collective-permute-start(f32[45,8,128]{2,1,0:T(8,128)S(1)} %get-tuple-element.12), channel_id=1, source_target_pairs={{0,2},{2,0},{4,6},{6,4},{8,10},{10,8},{12,14},{14,12},{1,3},{3,1},... | collective-permute-start | bytes 552968 | tf_op jit(solution)/shard_map/ppermute | solution.py:340
  20.9 6.9 %collective-permute-start.1 = (f32[45,8,128]{2,1,0:T(8,128)S(1)}, f32[45,8,128]{2,1,0:T(8,128)S(1)}, u32[]{:S(2)}, u32[]{:S(2)}) collective-permute-start(f32[45,8,128]{2,1,0:T(8,128)S(1)} %get-tuple-element.13), channel_id=1, source_target_pairs={{2,4},{4,2},{6,8},{8,6},{10,12},{12,10},{3,5},{5,3},{7,9},{9,7},{1... | collective-permute-start | bytes 552968 | tf_op jit(solution)/shard_map/ppermute | solution.py:341
  23.3 6.7 %copy-start.3 = (f32[128,128]{1,0:T(8,128)S(1)}, f32[128,128]{1,0:T(8,128)}, u32[]{:S(2)}) copy-start(f32[128,128]{1,0:T(8,128)} %constant.13.clone.weigh) | copy-start | bytes 196612
  23.3 7.9 %collective-permute-start.4 = (f32[8,768]{1,0:T(8,128)S(1)}, f32[8,768]{1,0:T(8,128)S(1)}, u32[]{:S(2)}, u32[]{:S(2)}) collective-permute-start(f32[8,768]{1,0:T(8,128)S(1)} %get-tuple-element.18), channel_id=1, source_target_pairs={{16,0},{32,16},{48,32},{64,48},{80,64},{96,80},{112,96},{128,112},... | collective-permute-start | bytes 73736 | tf_op jit(solution)/shard_map/ppermute | solution.py:345
  27.5 6.1 %collective-permute-start.3 = (f32[8,768]{1,0:T(8,128)S(1)}, f32[8,768]{1,0:T(8,128)S(1)}, u32[]{:S(2)}, u32[]{:S(2)}) collective-permute-start(f32[8,768]{1,0:T(8,128)S(1)} %get-tuple-element.18), channel_id=1, source_target_pairs={{0,16},{16,32},{32,48},{48,64},{64,80},{80,96},{96,112},{112,128},... | collective-permute-start | bytes 73736 | tf_op jit(solution)/shard_map/ppermute | solution.py:344
  27.7 2.3 %copy-start.6 = (f32[16,128]{1,0:T(8,128)S(1)}, f32[16,128]{1,0:T(8,128)}, u32[]{:S(2)}) copy-start(f32[16,128]{1,0:T(8,128)} %constant.14.clone.powers) | copy-start | bytes 24580
  33.6 16.9 %copy-start.5 = (f32[24,256]{1,0:T(8,128)S(1)}, f32[24,256]{1,0:T(8,128)}, u32[]{:S(2)}) copy-start(f32[24,256]{1,0:T(8,128)} %constant.12.clone.side) | copy-start | bytes 73732

commit v5 on v4

--- a/solution.py
+++ b/solution.py
@@ -126,12 +126,7 @@
         copy.wait()
 
 
-def pack_kernel(shifts, density, moments, pick, inside, outside, cols, turns, flux):
-    axial, place = lax.axis_index("axial"), lax.axis_index("pitch")
-    extent = WIDTH * RING
-    for j in range(PIECE):
-        shift = shifts[lax.rem(place * PIECE + j, INST)]
-        turns[j] = jnp.where(axial == 1, shift, (extent - shift) & (extent - 1))
+def pack_kernel(density, moments, pick, inside, outside, cols, flux):
     even = lax.rem(lax.axis_index("radial"), 2) == 0
     low = row_index((INST, ROWS, WIDTH)) < 4
     for v in range(VARS):
@@ -204,12 +199,20 @@
                 total = total + weight * (back - forth)
             added.append(total)
         put(rest, a, added)
-    through = dot(flux[...], local[:, 0 : 2 * WIDTH], ((1,), (0,)))
+    through = dot3(flux[...], local[:, 0 : 2 * WIDTH], ((1,), (0,)))
     res[...] = rest[...] + through[:, 0:WIDTH]
-    upd[...] = through[:, WIDTH:] + dot(rest[...], local[:, 2 * WIDTH :], ((1,), (0,)))
-    sums[...] = dot(pick[0:8], flux[...], ((1,), (1,))) + dot(
+    upd[...] = through[:, WIDTH:] + dot3(rest[...], local[:, 2 * WIDTH :], ((1,), (0,)))
+    sums[...] = dot3(pick[0:8], flux[...], ((1,), (1,))) + dot3(
         pick[8:16], rest[...], ((1,), (1,))
     )
+
+
+def turn_kernel(shifts, turns):
+    axial, place = lax.axis_index("axial"), lax.axis_index("pitch")
+    extent = WIDTH * RING
+    for j in range(PIECE):
+        shift = shifts[lax.rem(place * PIECE + j, INST)]
+        turns[j] = jnp.where(axial == 1, shift, (extent - shift) & (extent - 1))
 
 
 def align_kernel(turns, whole, sums, weigh, powers, out, rolled, kept):
@@ -318,22 +321,20 @@
     )(*[pltpu.with_memory_space_constraint(x, pltpu.HBM) for x in (density, moments)])
     across = lax.ppermute(facing, "axial", [(0, 1), (1, 0)])
     vmem = pl.BlockSpec(memory_space=pltpu.VMEM)
-    smem = pl.BlockSpec(memory_space=pltpu.SMEM)
     halo = jax.ShapeDtypeStruct((PAIRS, ROWS, WIDTH), jnp.float32)
-    inside, outside, cols, turns = pl.pallas_call(
+    inside, outside, cols = pl.pallas_call(
         pack_kernel,
         out_shape=[
             halo,
             halo,
             jax.ShapeDtypeStruct((8, height), jnp.float32),
-            jax.ShapeDtypeStruct((PIECE,), jnp.int32),
         ],
-        in_specs=[smem, vmem, vmem, vmem],
-        out_specs=[vmem, vmem, vmem, smem],
+        in_specs=[vmem] * 3,
+        out_specs=[vmem] * 3,
         scratch_shapes=[pltpu.VMEM((height, WIDTH), jnp.float32)],
         cost_estimate=pl.CostEstimate(flops=10**6, bytes_accessed=10**6, transcendentals=0),
         compiler_params=pltpu.CompilerParams(vmem_limit_bytes=GRANT),
-    )(shifts, density, moments, pick)
+    )(density, moments, pick)
     count_r = lax.axis_size("radial")
     pairs = [(i, i ^ 1) for i in range(count_r)]
     between = [(i, i - 1 if i % 2 == 0 else i + 1) for i in range(1, count_r - 1)]
@@ -351,6 +352,14 @@
         inputs=6,
         work=(10**8, 2 * 10**6),
     )(density, moments, inside, outside, local, pick)
+    smem = pl.BlockSpec(memory_space=pltpu.SMEM)
+    turns = pl.pallas_call(
+        turn_kernel,
+        out_shape=jax.ShapeDtypeStruct((PIECE,), jnp.int32),
+        in_specs=[smem],
+        out_specs=smem,
+        compiler_params=pltpu.CompilerParams(vmem_limit_bytes=GRANT),
+    )(shifts)
     (send,) = call(
         align_kernel,
         [(RING * SENT, WIDTH)],

time: 52.4 us -> 50.9 us (0.971)
  blocking collectives: 16.9 us -> 16.1 us
    pallas_call x0 -> x1, Pallas kernels: none -> 1.16 us  [local_step(): pl.pallas_call(turn_kernel, out_shape=jax.ShapeDtypeStruct((PIECE,), jnp....]
    pallas_call x1, Pallas kernels: 2.33 us -> 1.44 us  [local_step(): call(main_kernel, [(height, WIDTH), (height, WIDTH), (8, height)], scratc...]
    all_to_all x1, blocking collectives: 16.9 us -> 16.1 us  [local_step(): got = lax.all_to_all(send.reshape(RING, SENT // 4, 4, WIDTH), 'pitch', 0, 0)]
    pallas_call x1, Pallas kernels: 1.19 us -> 0.55 us  [local_step(): pl.pallas_call(pack_kernel, out_shape=[halo, halo, jax.ShapeDtypeStruct((...]
  transfers between devices with their start and end apart: 6 -> 6, of which waited for: 3 -> 2; matrix products, arithmetic and copies ran while one was open for 0% -> 0% of each run, Pallas kernels for 9% -> 9%
where the time goes in v5:
time: 50.9 us; the launch traced here: 50.4 us
  starting transfers between devices  19.5 us (38%)
  blocking collectives  16.1 us (32%)
  waiting for transfers between devices  7.41 us (15%)
  Pallas kernels  6.6 us (13%)
  between operations  0.8 us (2%)
    all_to_all x1, blocking collectives, local_step(): got = lax.all_to_all(send.reshape(RING, SENT // 4, 4, WIDTH), 'pitch', 0, 0)  16.1 us
    all_to_all x1, starting transfers between devices, local_step(): lax.all_to_all(across.reshape(RING, PIECE, ROWS, WIDTH), 'pitch', 0, 0)  9.63 us
    ppermute x1, waiting for transfers between devices, local_step(): across = lax.ppermute(facing, 'axial', [(0, 1), (1, 0)])  5.23 us
    ppermute x1, starting transfers between devices, local_step(): right = lax.ppermute(cols, 'pitch', back)  4.11 us
    ppermute x1, starting transfers between devices, local_step(): across = lax.ppermute(facing, 'axial', [(0, 1), (1, 0)])  3.11 us
    ppermute x1, starting transfers between devices, local_step(): outside = lax.ppermute(outside, 'radial', between)  2.6 us
    ppermute x1, waiting for transfers between devices, local_step(): left = lax.ppermute(cols, 'pitch', ring)  2.18 us
    pallas_call x1, Pallas kernels, local_step(): call(main_kernel, [(height, WIDTH), (height, WIDTH), (8, height)], scratc...  1.44 us
  transfers between devices with their start and end apart: 6, of which 2 were waited for; matrix products, arithmetic and copies ran while one was open for 0% of the time, Pallas kernels for 9%

profile of v5, /device:TPU:8, one launch (start us, length us, event | category | flops | bytes accessed | tf_op | source)
XLA Modules:
  0.0 50.4 jit_solution(17518102062129559814)
XLA Ops:
  0.6 0.9 %shard_map.98 = f32[48,8,128]{2,1,0:T(8,128)S(1)} custom-call(f32[9,2,8,128]{3,2,1,0:T(8,128)} %density.5, f32[9,4,2,8,128]{4,3,2,1,0:T(8,128)} %moments.5), custom_call_target="tpu_custom_call" | custom-call | tf_op jit(solution)/shard_map/pallas_call | solution.py:314
  1.5 0.0 copy-start
  1.5 3.1 %collective-permute-start.2 = (f32[48,8,128]{2,1,0:T(8,128)S(1)}, f32[48,8,128]{2,1,0:T(8,128)}, u32[]{:S(2)}, u32[]{:S(2)}) collective-permute-start(f32[48,8,128]{2,1,0:T(8,128)S(1)} %shard_map.98), channel_id=1, source_target_pairs={{0,1},{1,0},{2,3},{3,2},{4,5},{5,4},{6,7},{7,6},{8,9},{9,8},{10,11... | collective-permute-start | bytes 589832 | tf_op jit(solution)/shard_map/ppermute | solution.py:322
  4.7 5.2 %collective-permute-done.2 = f32[48,8,128]{2,1,0:T(8,128)} collective-permute-done((f32[48,8,128]{2,1,0:T(8,128)S(1)}, f32[48,8,128]{2,1,0:T(8,128)}, u32[]{:S(2)}, u32[]{:S(2)}) %collective-permute-start.2) | collective-permute-done | bytes 196640 | tf_op jit(solution)/shard_map/ppermute | solution.py:322
  9.9 0.0 copy-start.2
  9.9 0.0 copy-start.4
  9.9 9.6 %all-to-all-start = ((f32[16,3,8,128]{3,2,1,0:T(8,128)}), f32[16,3,8,128]{3,2,1,0:T(8,128)S(1)}, u32[]{:S(2)}, u32[]{:S(2)}) async-start(f32[16,3,8,128]{3,2,1,0:T(8,128)} %bitcast), calls=%async_computation | async-start | bytes 393216 | tf_op jit(solution)/shard_map/all_to_all | solution.py:347
  19.5 0.0 copy-done
  19.5 0.0 copy-done.2
  19.5 0.0 copy-done.4
  19.6 0.0 copy-start.1
  19.6 0.5 %shard_map.95 = (f32[45,8,128]{2,1,0:T(8,128)S(1)}, f32[45,8,128]{2,1,0:T(8,128)S(1)}, f32[8,768]{1,0:T(8,128)S(1)}) custom-call(f32[9,2,8,128]{3,2,1,0:T(8,128)S(1)} %copy-done.2, f32[9,4,2,8,128]{4,3,2,1,0:T(8,128)S(1)} %copy-done, f32[16,128]{1,0:T(8,128)S(1)} %copy-done.4), custom_call_target="tpu_custom_call" | custom-call | flops 1000000 | bytes 1000000 | tf_op jit(solution)/shard_map/pallas_call | solution.py:325
  20.1 0.0 collective-permute-start
  20.1 0.0 copy-start.7
  20.1 2.6 %collective-permute-start.1 = (f32[45,8,128]{2,1,0:T(8,128)S(1)}, f32[45,8,128]{2,1,0:T(8,128)S(1)}, u32[]{:S(2)}, u32[]{:S(2)}) collective-permute-start(f32[45,8,128]{2,1,0:T(8,128)S(1)} %get-tuple-element.12), channel_id=1, source_target_pairs={{2,4},{4,2},{6,8},{8,6},{10,12},{12,10},{3,5},{5,3},{7,9},{9,7},{1... | collective-permute-start | bytes 552968 | tf_op jit(solution)/shard_map/ppermute | solution.py:342
  22.7 4.1 %collective-permute-start.4 = (f32[8,768]{1,0:T(8,128)S(1)}, f32[8,768]{1,0:T(8,128)S(1)}, u32[]{:S(2)}, u32[]{:S(2)}) collective-permute-start(f32[8,768]{1,0:T(8,128)S(1)} %get-tuple-element.16), channel_id=1, source_target_pairs={{16,0},{32,16},{48,32},{64,48},{80,64},{96,80},{112,96},{128,112},... | collective-permute-start | bytes 73736 | tf_op jit(solution)/shard_map/ppermute | solution.py:346
  26.9 0.0 collective-permute-start.3
  26.9 0.0 copy-done.7
  26.9 1.2 %shard_map.97.turns = s32[3]{0:T(128)S(1)} custom-call(s32[9]{0:T(128)S(1)} %copy-done.7), custom_call_target="tpu_custom_call" | custom-call | tf_op jit(solution)/shard_map/pallas_call | solution.py:356
  28.0 0.0 copy-start.3
  28.0 0.0 copy-start.6
  28.0 0.0 collective-permute-done.inside
  28.1 0.0 collective-permute-done.1.outside
  28.1 0.0 copy-done.1
  28.1 1.4 %shard_map.96 = (f32[768,128]{1,0:T(8,128)S(1)}, f32[768,128]{1,0:T(8,128)S(1)}, f32[8,768]{1,0:T(8,128)S(1)}) custom-call(f32[9,2,8,128]{3,2,1,0:T(8,128)S(1)} %copy-done.2, f32[9,4,2,8,128]{4,3,2,1,0:T(8,128)S(1)} %copy-done, f32[45,8,128]{2,1,0:T(8,128)S(1)} %collective-permute-done.inside, f32[45,8,128]{2,1,0:T(8,128)S(1)} %collective-permute-done.1.outside, ...), custom_call_target="tpu_custom_call" | custom-call | flops 100000000 | bytes 2000000 | tf_op jit(solution)/shard_map/pallas_call | solution.py:348
  29.5 0.0 all-to-all-done.whole
  29.5 0.0 copy-done.3
  29.5 0.0 copy-done.6
  29.6 1.2 %shard_map.99 = f32[576,128]{1,0:T(8,128)S(1)} custom-call(s32[3]{0:T(128)S(1)} %shard_map.97.turns, f32[16,3,8,128]{3,2,1,0:T(8,128)S(1)} %all-to-all-done.whole, f32[8,768]{1,0:T(8,128)S(1)} %get-tuple-element.15.sums, f32[128,128]{1,0:T(8,128)S(1)} %copy-done.3, f32[16,128]{1,0:T(8,128)S(1)} %copy-done.6), custom_call_target="tpu_custom_call" | custom-call | flops 10000000 | bytes 1000000 | tf_op jit(solution)/shard_map/pallas_call | solution.py:363
  30.7 0.0 collective-permute-done.4.right
  30.8 2.2 %collective-permute-done.3.left = f32[8,768]{1,0:T(8,128)S(1)} collective-permute-done((f32[8,768]{1,0:T(8,128)S(1)}, f32[8,768]{1,0:T(8,128)S(1)}, u32[]{:S(2)}, u32[]{:S(2)}) %collective-permute-start.3) | collective-permute-done | bytes 24608 | tf_op jit(solution)/shard_map/ppermute | solution.py:345
  32.9 0.0 copy-start.5
  32.9 16.1 %all_to_all.10 = f32[16,9,4,128]{3,2,1,0:T(4,128)S(1)} all-to-all(f32[16,9,4,128]{3,2,1,0:T(4,128)S(1)} %bitcast.3), channel_id=1, replica_groups=mesh['pitch'=16,'radial'=8,'axial'=2] {'pitch'}, dimensions={0} | all-to-all | bytes 589824 | tf_op jit(solution)/shard_map/all_to_all | solution.py:372
  49.0 0.0 copy-done.5
  49.0 1.4 %shard_map.100 = (f32[9,5,2,8,128]{4,3,2,1,0:T(8,128)}, f32[9,5,2,8,128]{4,3,2,1,0:T(8,128)}) custom-call(f32[768,128]{1,0:T(8,128)S(1)} %get-tuple-element.13.res, f32[768,128]{1,0:T(8,128)S(1)} %get-tuple-element.14.upd, f32[576,128]{1,0:T(8,128)S(1)} %bitcast.4, f32[8,768]{1,0:T(8,128)S(1)} %collective-permute-done.3.left, ...), custom_call_target="tpu_custom_call" | custom-call | flops 10000000 | bytes 2000000 | tf_op jit(solution)/shard_map/pallas_call | solution.py:376
Async XLA Ops:
  1.5 18.0 %copy-start = (f32[9,4,2,8,128]{4,3,2,1,0:T(8,128)S(1)}, f32[9,4,2,8,128]{4,3,2,1,0:T(8,128)}, u32[]{:S(2)}) copy-start(f32[9,4,2,8,128]{4,3,2,1,0:T(8,128)} %moments.5) | copy-start | bytes 884740
  1.5 8.3 %collective-permute-start.2 = (f32[48,8,128]{2,1,0:T(8,128)S(1)}, f32[48,8,128]{2,1,0:T(8,128)}, u32[]{:S(2)}, u32[]{:S(2)}) collective-permute-start(f32[48,8,128]{2,1,0:T(8,128)S(1)} %shard_map.98), channel_id=1, source_target_pairs={{0,1},{1,0},{2,3},{3,2},{4,5},{5,4},{6,7},{7,6},{8,9},{9,8},{10,11... | collective-permute-start | bytes 589832 | tf_op jit(solution)/shard_map/ppermute | solution.py:322
  9.9 9.7 %copy-start.2 = (f32[9,2,8,128]{3,2,1,0:T(8,128)S(1)}, f32[9,2,8,128]{3,2,1,0:T(8,128)}, u32[]{:S(2)}) copy-start(f32[9,2,8,128]{3,2,1,0:T(8,128)} %density.5) | copy-start | bytes 221188
  9.9 9.7 %copy-start.4 = (f32[16,128]{1,0:T(8,128)S(1)}, f32[16,128]{1,0:T(8,128)}, u32[]{:S(2)}) copy-start(f32[16,128]{1,0:T(8,128)} %constant.11.clone.pick) | copy-start | bytes 24580
  9.9 19.6 %all-to-all-start = ((f32[16,3,8,128]{3,2,1,0:T(8,128)}), f32[16,3,8,128]{3,2,1,0:T(8,128)S(1)}, u32[]{:S(2)}, u32[]{:S(2)}) async-start(f32[16,3,8,128]{3,2,1,0:T(8,128)} %bitcast), calls=%async_computation | async-start | bytes 393216 | tf_op jit(solution)/shard_map/all_to_all | solution.py:347
  19.6 8.5 %copy-start.1 = (f32[128,384]{1,0:T(8,128)S(1)}, f32[128,384]{1,0:T(8,128)}, u32[]{:S(2)}) copy-start(f32[128,384]{1,0:T(8,128)} %constant.10.clone.local) | copy-start | bytes 589828
  20.1 7.9 %collective-permute-start = (f32[45,8,128]{2,1,0:T(8,128)S(1)}, f32[45,8,128]{2,1,0:T(8,128)S(1)}, u32[]{:S(2)}, u32[]{:S(2)}) collective-permute-start(f32[45,8,128]{2,1,0:T(8,128)S(1)} %get-tuple-element.11), channel_id=1, source_target_pairs={{0,2},{2,0},{4,6},{6,4},{8,10},{10,8},{12,14},{14,12},{1,3},{3,1},... | collective-permute-start | bytes 552968 | tf_op jit(solution)/shard_map/ppermute | solution.py:341
  20.1 6.7 %copy-start.7 = (s32[9]{0:T(128)S(1)}, s32[9]{0:T(128)}, u32[]{:S(2)}) copy-start(s32[9]{0:T(128)} %shifts.1) | copy-start | bytes 112
  20.1 7.9 %collective-permute-start.1 = (f32[45,8,128]{2,1,0:T(8,128)S(1)}, f32[45,8,128]{2,1,0:T(8,128)S(1)}, u32[]{:S(2)}, u32[]{:S(2)}) collective-permute-start(f32[45,8,128]{2,1,0:T(8,128)S(1)} %get-tuple-element.12), channel_id=1, source_target_pairs={{2,4},{4,2},{6,8},{8,6},{10,12},{12,10},{3,5},{5,3},{7,9},{9,7},{1... | collective-permute-start | bytes 552968 | tf_op jit(solution)/shard_map/ppermute | solution.py:342
  22.7 8.0 %collective-permute-start.4 = (f32[8,768]{1,0:T(8,128)S(1)}, f32[8,768]{1,0:T(8,128)S(1)}, u32[]{:S(2)}, u32[]{:S(2)}) collective-permute-start(f32[8,768]{1,0:T(8,128)S(1)} %get-tuple-element.16), channel_id=1, source_target_pairs={{16,0},{32,16},{48,32},{64,48},{80,64},{96,80},{112,96},{128,112},... | collective-permute-start | bytes 73736 | tf_op jit(solution)/shard_map/ppermute | solution.py:346
  26.9 6.1 %collective-permute-start.3 = (f32[8,768]{1,0:T(8,128)S(1)}, f32[8,768]{1,0:T(8,128)S(1)}, u32[]{:S(2)}, u32[]{:S(2)}) collective-permute-start(f32[8,768]{1,0:T(8,128)S(1)} %get-tuple-element.16), channel_id=1, source_target_pairs={{0,16},{16,32},{32,48},{48,64},{64,80},{80,96},{96,112},{112,128},... | collective-permute-start | bytes 73736 | tf_op jit(solution)/shard_map/ppermute | solution.py:345
  28.0 1.5 %copy-start.3 = (f32[128,128]{1,0:T(8,128)S(1)}, f32[128,128]{1,0:T(8,128)}, u32[]{:S(2)}) copy-start(f32[128,128]{1,0:T(8,128)} %constant.13.clone.weigh) | copy-start | bytes 196612
  28.0 1.5 %copy-start.6 = (f32[16,128]{1,0:T(8,128)S(1)}, f32[16,128]{1,0:T(8,128)}, u32[]{:S(2)}) copy-start(f32[16,128]{1,0:T(8,128)} %constant.14.clone.powers) | copy-start | bytes 24580
  32.9 16.1 %copy-start.5 = (f32[24,256]{1,0:T(8,128)S(1)}, f32[24,256]{1,0:T(8,128)}, u32[]{:S(2)}) copy-start(f32[24,256]{1,0:T(8,128)} %constant.12.clone.side) | copy-start | bytes 73732

commit v6 on v4

--- a/solution.py
+++ b/solution.py
@@ -263,15 +263,22 @@
     for h in range(1, RING):
         carries = carries + got[h * SENT + tall : (h + 1) * SENT]
     line = row_index((8, WIDTH))
+    pair = jnp.concatenate(
+        [
+            jnp.where(
+                line == 0, carries[t : t + 1], jnp.where(line == 1, carries[6 + t : 7 + t], 0.0)
+            )
+            for t in range(6)
+        ],
+        axis=1,
+    )
+    sides = jnp.concatenate([left[...], right[...], pair], axis=0)
+    whole = dot3(sides, side[...], ((0,), (0,)))
     copies = []
     for t in range(6):
         a, part = t // 3, t % 3
         at = slice(t * WIDTH, (t + 1) * WIDTH)
-        pair = jnp.where(
-            line == 0, carries[t : t + 1], jnp.where(line == 1, carries[6 + t : 7 + t], 0.0)
-        )
-        sides = jnp.concatenate([left[:, at], right[:, at], pair], axis=0)
-        added = dot3(sides, side[...], ((0,), (0,)))
+        added = whole[at]
         mine = axial == 1 - a
         here = slice(part * WIDTH, (part + 1) * WIDTH)
         r = res[at] + added[:, 0:WIDTH] + jnp.where(mine, windows[here], 0.0)

time: 52.4 us -> 52.4 us (level)
  no operation moved by 1% of the time
where the time goes in v6:
time: 52.4 us; the launch traced here: 51.9 us
  starting transfers between devices  19.4 us (37%)
  blocking collectives  16.9 us (32%)
  waiting for transfers between devices  7.78 us (15%)
  Pallas kernels  7.02 us (13%)
  between operations  0.76 us (1%)
    all_to_all x1, blocking collectives, local_step(): got = lax.all_to_all(send.reshape(RING, SENT // 4, 4, WIDTH), 'pitch', 0, 0)  16.9 us
    all_to_all x1, starting transfers between devices, local_step(): lax.all_to_all(across.reshape(RING, PIECE, ROWS, WIDTH), 'pitch', 0, 0)  9.63 us
    ppermute x1, waiting for transfers between devices, local_step(): across = lax.ppermute(facing, 'axial', [(0, 1), (1, 0)])  5.23 us
    ppermute x1, starting transfers between devices, local_step(): right = lax.ppermute(cols, 'pitch', back)  4.11 us
    ppermute x1, starting transfers between devices, local_step(): across = lax.ppermute(facing, 'axial', [(0, 1), (1, 0)])  3.11 us
    ppermute x1, starting transfers between devices, local_step(): outside = lax.ppermute(outside, 'radial', between)  2.45 us
    pallas_call x1, Pallas kernels, local_step(): call(main_kernel, [(height, WIDTH), (height, WIDTH), (8, height)], scratc...  2.33 us
    ppermute x1, waiting for transfers between devices, local_step(): left = lax.ppermute(cols, 'pitch', ring)  2.27 us
  transfers between devices with their start and end apart: 6, of which 3 were waited for; matrix products, arithmetic and copies ran while one was open for 0% of the time, Pallas kernels for 9%

profile of v6, /device:TPU:8, one launch (start us, length us, event | category | flops | bytes accessed | tf_op | source)
XLA Modules:
  0.0 51.9 jit_solution(15238781394657734650)
XLA Ops:
  0.6 0.9 %shard_map.97 = f32[48,8,128]{2,1,0:T(8,128)S(1)} custom-call(f32[9,2,8,128]{3,2,1,0:T(8,128)} %density.5, f32[9,4,2,8,128]{4,3,2,1,0:T(8,128)} %moments.5), custom_call_target="tpu_custom_call" | custom-call | tf_op jit(solution)/shard_map/pallas_call | solution.py:318
  1.5 0.0 copy-start
  1.5 3.1 %collective-permute-start.2 = (f32[48,8,128]{2,1,0:T(8,128)S(1)}, f32[48,8,128]{2,1,0:T(8,128)}, u32[]{:S(2)}, u32[]{:S(2)}) collective-permute-start(f32[48,8,128]{2,1,0:T(8,128)S(1)} %shard_map.97), channel_id=1, source_target_pairs={{0,1},{1,0},{2,3},{3,2},{4,5},{5,4},{6,7},{7,6},{8,9},{9,8},{10,11... | collective-permute-start | bytes 589832 | tf_op jit(solution)/shard_map/ppermute | solution.py:326
  4.7 5.2 %collective-permute-done.2 = f32[48,8,128]{2,1,0:T(8,128)} collective-permute-done((f32[48,8,128]{2,1,0:T(8,128)S(1)}, f32[48,8,128]{2,1,0:T(8,128)}, u32[]{:S(2)}, u32[]{:S(2)}) %collective-permute-start.2) | collective-permute-done | bytes 196640 | tf_op jit(solution)/shard_map/ppermute | solution.py:326
  9.9 0.0 copy-start.2
  9.9 0.0 copy-start.4
  9.9 0.0 copy-start.7
  9.9 9.6 %all-to-all-start = ((f32[16,3,8,128]{3,2,1,0:T(8,128)}), f32[16,3,8,128]{3,2,1,0:T(8,128)S(1)}, u32[]{:S(2)}, u32[]{:S(2)}) async-start(f32[16,3,8,128]{3,2,1,0:T(8,128)} %bitcast), calls=%async_computation | async-start | bytes 393216 | tf_op jit(solution)/shard_map/all_to_all | solution.py:353
  19.5 0.0 copy-done
  19.5 0.0 copy-done.2
  19.5 0.0 copy-done.4
  19.6 0.0 copy-done.7
  19.6 0.0 copy-start.1
  19.6 1.2 %shard_map.95 = (f32[45,8,128]{2,1,0:T(8,128)S(1)}, f32[45,8,128]{2,1,0:T(8,128)S(1)}, f32[8,768]{1,0:T(8,128)S(1)}, s32[3]{0:T(128)S(1)}) custom-call(s32[9]{0:T(128)S(1)} %copy-done.7, f32[9,2,8,128]{3,2,1,0:T(8,128)S(1)} %copy-done.2, f32[9,4,2,8,128]{4,3,2,1,0:T(8,128)S(1)} %copy-done, f32[16,128]{1,0:T(8,128)S(1)} %copy-done.4), custom_call_target="tpu_custom_call" | custom-call | flops 1000000 | bytes 1000000 | tf_op jit(solution)/shard_map/pallas_call | solution.py:330
  20.8 0.1 collective-permute-start
  20.9 2.4 %collective-permute-start.1 = (f32[45,8,128]{2,1,0:T(8,128)S(1)}, f32[45,8,128]{2,1,0:T(8,128)S(1)}, u32[]{:S(2)}, u32[]{:S(2)}) collective-permute-start(f32[45,8,128]{2,1,0:T(8,128)S(1)} %get-tuple-element.13), channel_id=1, source_target_pairs={{2,4},{4,2},{6,8},{8,6},{10,12},{12,10},{3,5},{5,3},{7,9},{9,7},{1... | collective-permute-start | bytes 552968 | tf_op jit(solution)/shard_map/ppermute | solution.py:348
  23.3 0.0 copy-start.3
  23.3 4.1 %collective-permute-start.4 = (f32[8,768]{1,0:T(8,128)S(1)}, f32[8,768]{1,0:T(8,128)S(1)}, u32[]{:S(2)}, u32[]{:S(2)}) collective-permute-start(f32[8,768]{1,0:T(8,128)S(1)} %get-tuple-element.18), channel_id=1, source_target_pairs={{16,0},{32,16},{48,32},{64,48},{80,64},{96,80},{112,96},{128,112},... | collective-permute-start | bytes 73736 | tf_op jit(solution)/shard_map/ppermute | solution.py:352
  27.5 0.0 collective-permute-start.3
  27.5 0.0 collective-permute-done.inside
  27.5 0.3 collective-permute-done.1.outside
  27.7 0.0 copy-done.1
  27.7 0.0 copy-start.6
  27.7 2.3 %shard_map.96 = (f32[768,128]{1,0:T(8,128)S(1)}, f32[768,128]{1,0:T(8,128)S(1)}, f32[8,768]{1,0:T(8,128)S(1)}) custom-call(f32[9,2,8,128]{3,2,1,0:T(8,128)S(1)} %copy-done.2, f32[9,4,2,8,128]{4,3,2,1,0:T(8,128)S(1)} %copy-done, f32[45,8,128]{2,1,0:T(8,128)S(1)} %collective-permute-done.inside, f32[45,8,128]{2,1,0:T(8,128)S(1)} %collective-permute-done.1.outside, ...), custom_call_target="tpu_custom_call" | custom-call | flops 100000000 | bytes 2000000 | tf_op jit(solution)/shard_map/pallas_call | solution.py:354
  30.1 0.0 all-to-all-done.whole
  30.1 0.0 copy-done.3
  30.1 0.0 copy-done.6
  30.1 1.2 %shard_map.98 = f32[576,128]{1,0:T(8,128)S(1)} custom-call(s32[3]{0:T(128)S(1)} %get-tuple-element.16.turns, f32[16,3,8,128]{3,2,1,0:T(8,128)S(1)} %all-to-all-done.whole, f32[8,768]{1,0:T(8,128)S(1)} %get-tuple-element.17.sums, f32[128,128]{1,0:T(8,128)S(1)} %copy-done.3, f32[16,128]{1,0:T(8,128)S(1)} %copy-done.6), custom_call_target="tpu_custom_call" | custom-call | flops 10000000 | bytes 1000000 | tf_op jit(solution)/shard_map/pallas_call | solution.py:361
  31.3 0.0 collective-permute-done.4.right
  31.3 2.3 %collective-permute-done.3.left = f32[8,768]{1,0:T(8,128)S(1)} collective-permute-done((f32[8,768]{1,0:T(8,128)S(1)}, f32[8,768]{1,0:T(8,128)S(1)}, u32[]{:S(2)}, u32[]{:S(2)}) %collective-permute-start.3) | collective-permute-done | bytes 24608 | tf_op jit(solution)/shard_map/ppermute | solution.py:351
  33.6 0.0 copy-start.5
  33.6 16.9 %all_to_all.10 = f32[16,9,4,128]{3,2,1,0:T(4,128)S(1)} all-to-all(f32[16,9,4,128]{3,2,1,0:T(4,128)S(1)} %bitcast.3), channel_id=1, replica_groups=mesh['pitch'=16,'radial'=8,'axial'=2] {'pitch'}, dimensions={0} | all-to-all | bytes 589824 | tf_op jit(solution)/shard_map/all_to_all | solution.py:370
  50.5 0.0 copy-done.5
  50.5 1.4 %shard_map.99 = (f32[9,5,2,8,128]{4,3,2,1,0:T(8,128)}, f32[9,5,2,8,128]{4,3,2,1,0:T(8,128)}) custom-call(f32[768,128]{1,0:T(8,128)S(1)} %get-tuple-element.14.res, f32[768,128]{1,0:T(8,128)S(1)} %get-tuple-element.15.upd, f32[576,128]{1,0:T(8,128)S(1)} %bitcast.4, f32[8,768]{1,0:T(8,128)S(1)} %collective-permute-done.3.left, ...), custom_call_target="tpu_custom_call" | custom-call | flops 10000000 | bytes 2000000 | tf_op jit(solution)/shard_map/pallas_call | solution.py:374
Async XLA Ops:
  1.5 18.0 %copy-start = (f32[9,4,2,8,128]{4,3,2,1,0:T(8,128)S(1)}, f32[9,4,2,8,128]{4,3,2,1,0:T(8,128)}, u32[]{:S(2)}) copy-start(f32[9,4,2,8,128]{4,3,2,1,0:T(8,128)} %moments.5) | copy-start | bytes 884740
  1.5 8.3 %collective-permute-start.2 = (f32[48,8,128]{2,1,0:T(8,128)S(1)}, f32[48,8,128]{2,1,0:T(8,128)}, u32[]{:S(2)}, u32[]{:S(2)}) collective-permute-start(f32[48,8,128]{2,1,0:T(8,128)S(1)} %shard_map.97), channel_id=1, source_target_pairs={{0,1},{1,0},{2,3},{3,2},{4,5},{5,4},{6,7},{7,6},{8,9},{9,8},{10,11... | collective-permute-start | bytes 589832 | tf_op jit(solution)/shard_map/ppermute | solution.py:326
  9.9 9.7 %copy-start.2 = (f32[9,2,8,128]{3,2,1,0:T(8,128)S(1)}, f32[9,2,8,128]{3,2,1,0:T(8,128)}, u32[]{:S(2)}) copy-start(f32[9,2,8,128]{3,2,1,0:T(8,128)} %density.5) | copy-start | bytes 221188
  9.9 9.7 %copy-start.4 = (f32[16,128]{1,0:T(8,128)S(1)}, f32[16,128]{1,0:T(8,128)}, u32[]{:S(2)}) copy-start(f32[16,128]{1,0:T(8,128)} %constant.11.clone.pick) | copy-start | bytes 24580
  9.9 9.7 %copy-start.7 = (s32[9]{0:T(128)S(1)}, s32[9]{0:T(128)}, u32[]{:S(2)}) copy-start(s32[9]{0:T(128)} %shifts.1) | copy-start | bytes 112
  9.9 20.2 %all-to-all-start = ((f32[16,3,8,128]{3,2,1,0:T(8,128)}), f32[16,3,8,128]{3,2,1,0:T(8,128)S(1)}, u32[]{:S(2)}, u32[]{:S(2)}) async-start(f32[16,3,8,128]{3,2,1,0:T(8,128)} %bitcast), calls=%async_computation | async-start | bytes 393216 | tf_op jit(solution)/shard_map/all_to_all | solution.py:353
  19.6 8.2 %copy-start.1 = (f32[128,384]{1,0:T(8,128)S(1)}, f32[128,384]{1,0:T(8,128)}, u32[]{:S(2)}) copy-start(f32[128,384]{1,0:T(8,128)} %constant.10.clone.local) | copy-start | bytes 589828
  20.8 6.7 %collective-permute-start = (f32[45,8,128]{2,1,0:T(8,128)S(1)}, f32[45,8,128]{2,1,0:T(8,128)S(1)}, u32[]{:S(2)}, u32[]{:S(2)}) collective-permute-start(f32[45,8,128]{2,1,0:T(8,128)S(1)} %get-tuple-element.12), channel_id=1, source_target_pairs={{0,2},{2,0},{4,6},{6,4},{8,10},{10,8},{12,14},{14,12},{1,3},{3,1},... | collective-permute-start | bytes 552968 | tf_op jit(solution)/shard_map/ppermute | solution.py:347
  20.9 6.9 %collective-permute-start.1 = (f32[45,8,128]{2,1,0:T(8,128)S(1)}, f32[45,8,128]{2,1,0:T(8,128)S(1)}, u32[]{:S(2)}, u32[]{:S(2)}) collective-permute-start(f32[45,8,128]{2,1,0:T(8,128)S(1)} %get-tuple-element.13), channel_id=1, source_target_pairs={{2,4},{4,2},{6,8},{8,6},{10,12},{12,10},{3,5},{5,3},{7,9},{9,7},{1... | collective-permute-start | bytes 552968 | tf_op jit(solution)/shard_map/ppermute | solution.py:348
  23.3 6.7 %copy-start.3 = (f32[128,128]{1,0:T(8,128)S(1)}, f32[128,128]{1,0:T(8,128)}, u32[]{:S(2)}) copy-start(f32[128,128]{1,0:T(8,128)} %constant.13.clone.weigh) | copy-start | bytes 196612
  23.3 7.9 %collective-permute-start.4 = (f32[8,768]{1,0:T(8,128)S(1)}, f32[8,768]{1,0:T(8,128)S(1)}, u32[]{:S(2)}, u32[]{:S(2)}) collective-permute-start(f32[8,768]{1,0:T(8,128)S(1)} %get-tuple-element.18), channel_id=1, source_target_pairs={{16,0},{32,16},{48,32},{64,48},{80,64},{96,80},{112,96},{128,112},... | collective-permute-start | bytes 73736 | tf_op jit(solution)/shard_map/ppermute | solution.py:352
  27.5 6.1 %collective-permute-start.3 = (f32[8,768]{1,0:T(8,128)S(1)}, f32[8,768]{1,0:T(8,128)S(1)}, u32[]{:S(2)}, u32[]{:S(2)}) collective-permute-start(f32[8,768]{1,0:T(8,128)S(1)} %get-tuple-element.18), channel_id=1, source_target_pairs={{0,16},{16,32},{32,48},{48,64},{64,80},{80,96},{96,112},{112,128},... | collective-permute-start | bytes 73736 | tf_op jit(solution)/shard_map/ppermute | solution.py:351
  27.7 2.3 %copy-start.6 = (f32[16,128]{1,0:T(8,128)S(1)}, f32[16,128]{1,0:T(8,128)}, u32[]{:S(2)}) copy-start(f32[16,128]{1,0:T(8,128)} %constant.14.clone.powers) | copy-start | bytes 24580
  33.6 16.9 %copy-start.5 = (f32[24,256]{1,0:T(8,128)S(1)}, f32[24,256]{1,0:T(8,128)}, u32[]{:S(2)}) copy-start(f32[24,256]{1,0:T(8,128)} %constant.12.clone.side) | copy-start | bytes 73732
